TPU v7x, 512 devices: a whole 4x8x8 slice. The times are simulated.
512 devices in a mesh: req: 64 (over z, x, core), mdl: 8 (over y).
Axes of the slice: x: 4, y: 8, z: 8, core: 2. Of those that a mesh axis runs over, the one named last changes fastest.
Arguments:
- hidden_in: bfloat16 [8192, 2048], P('req'), may hold values from -6 to 6
- z_weight: bfloat16 [2048, 4096], P('req', 'mdl'), may hold values from -0.125 to 0.125
- x_weight: bfloat16 [2048, 4096], P('req', 'mdl'), may hold values from -0.125 to 0.125
- state_proj: bfloat16 [2048, 256], P('req'), may hold values from -0.125 to 0.125
- step_weight: bfloat16 [2048, 64], P('req', 'mdl'), may hold values from -0.125 to 0.125
- step_bias: float32 [64], P('mdl'), may hold values from -4 to -1
- decay_log: float32 [64], P('mdl'), may hold values from -2 to 1
- skip_gain: float32 [64], P('mdl'), may hold values from 0.5 to 2
- conv_inner: float32 [4, 4096], P(None, 'mdl'), may hold values from -3 to 3
- conv_state: float32 [4, 256], replicated, may hold values from -3 to 3
- norm_gain: float32 [4096], P('mdl'), may hold values from 0.1 to 1.9
- out_weight: bfloat16 [4096, 2048], P('mdl', 'req'), may hold values from -0.09375 to 0.09375
- state_pool: float32 [512, 64, 64, 128], P('req', 'mdl'), may hold values from -2.4 to 2.4
- conv_pool_inner: bfloat16 [512, 3, 4096], P('req', None, 'mdl'), may hold values from -6 to 6
- conv_pool_state: bfloat16 [512, 3, 256], P('req'), may hold values from -6 to 6
- owner_dev: int32 [512], replicated, may hold values from 0 to 63, as said below
- state_page: int32 [512], replicated, may hold values from 0 to 7, as said below
- conv_page: int32 [512], replicated, may hold values from 0 to 7, as said below
- accepted: int32 [512], replicated, may hold values from 1 to 16
Outputs:
- mixed: bfloat16 [8192, 2048], P('req', 'mdl')
- new_states: float32 [512, 64, 64, 128], P('req', 'mdl')
- conv_inner_out: bfloat16 [512, 3, 4096], P('req', None, 'mdl')
- conv_state_out: bfloat16 [512, 3, 256], P('req')
Inputs may be any that keep to these rules, and one draw needn't show every extreme that they name: `owner_dev`: request r of device i = r // 8 has its owner among devices i to i + 7 along req, counted modulo the axis size; among the 8 requests of one device at most 2 name the same owner, and exactly 2 do for one owner; every owner is named by exactly 8 requests in all. `state_page`: the requests of one owner have distinct state slots. `conv_page`: the requests of one owner have distinct convolution pages.
All inputs are finite; a program needn't handle non-finite values.
Results may differ from a plain program's by a relative error of at most 0.0069.
Values may be sent and summed in bfloat16 or wider, within the bound.
A program may use at most 64 MiB of HBM per device.

v0:
```python
import jax
import jax.numpy as jnp
from jax import lax
from jax.sharding import PartitionSpec as P

KCONV = 4
CAP = 2
WINDOW = 8


HIGH = lax.Precision.HIGHEST
EPSILON = 1e-05


def from_behind(value, axis, steps):
    count = lax.axis_size(axis)
    pairs = [(source, (source + steps) % count) for source in range(count)]
    return lax.ppermute(value, axis, pairs)


def one_hot_apply(table, values, shape):
    flat = values.reshape(table.shape[1], -1)
    return (
        jnp.dot(table, flat, preferred_element_type=jnp.float32).astype(jnp.bfloat16).reshape(shape)
    )


def route_tables(owner_dev, state_page, conv_page, accepted, groups, per_dev, this_dev):
    owner_grid = owner_dev.reshape(groups, per_dev)
    home_grid = jnp.arange(groups, dtype=jnp.int32)[:, None]
    offset_grid = (owner_grid - home_grid + groups) % groups
    positions = jnp.arange(per_dev, dtype=jnp.int32)
    earlier = positions[None, :] < positions[:, None]
    pair_rank = jnp.sum((owner_grid[:, :, None] == owner_grid[:, None, :]) & earlier[None], axis=2)
    slot_grid = offset_grid * CAP + pair_rank
    send_at = lax.dynamic_slice_in_dim(slot_grid, this_dev, 1, 0)[0]
    buffer_rows = jnp.arange(WINDOW * CAP, dtype=jnp.int32)
    send_table = (buffer_rows[:, None] == send_at[None, :]).astype(jnp.bfloat16)
    arrive_at = slot_grid.reshape(-1)
    slot_match = (owner_dev[None, :] == this_dev) & (state_page[None, :] == positions[:, None])
    pick_from = jnp.sum(jnp.where(slot_match, arrive_at[None, :], 0), axis=1)
    conv_of = jnp.sum(jnp.where(slot_match, conv_page[None, :], 0), axis=1)
    kept_count = jnp.sum(jnp.where(slot_match, accepted[None, :], 0), axis=1)
    gather_table = (buffer_rows[None, :] == pick_from[:, None]).astype(jnp.bfloat16)
    place_table = (positions[:, None] == conv_of[None, :]).astype(jnp.bfloat16)
    return (send_table, gather_table, place_table, conv_of, kept_count)


def project_in(rows, z_weight, x_weight, state_proj, step_weight):
    pieces = (
        lax.all_gather(z_weight, "req", axis=0, tiled=True),
        lax.all_gather(x_weight, "req", axis=0, tiled=True),
        lax.all_gather(state_proj, "req", axis=0, tiled=True),
        lax.all_gather(step_weight, "req", axis=0, tiled=True),
    )
    gate_pre, inner_raw, state_full, step_raw = tuple(
        (jnp.dot(rows, piece, preferred_element_type=jnp.float32) for piece in pieces)
    )
    state_raw = state_full.astype(jnp.bfloat16)
    packed = jnp.concatenate([inner_raw.astype(jnp.bfloat16), state_raw], axis=1)
    return (gate_pre, packed, step_raw.astype(jnp.bfloat16))


def mix_requests(
    packed, step_raw, history, kernel, step_bias, decay_log, skip_gain, state_pool, kept_count
):
    per_dev, draft, channels = packed.shape
    heads, head_dim, state_width = (state_pool.shape[1], state_pool.shape[2], state_pool.shape[3])
    inner = heads * head_dim
    series = jnp.concatenate([history, packed], axis=1)
    series_f = series.astype(jnp.float32)
    conv_sum = kernel[0] * series_f[:, 0:draft]
    for tap in range(1, KCONV):
        conv_sum = conv_sum + kernel[tap] * series_f[:, tap : tap + draft]
    active = jax.nn.silu(conv_sum)
    inputs_x = active[:, :, :inner].reshape(per_dev, draft, heads, head_dim)
    b_rows = active[:, :, inner : inner + state_width]
    c_rows = active[:, :, inner + state_width :]
    step_size = jax.nn.softplus(step_raw.astype(jnp.float32) + step_bias)
    log_decay = jnp.cumsum(step_size * -jnp.exp(decay_log), axis=1)
    step_order = jnp.arange(draft, dtype=jnp.int32)
    causal = (step_order[None, :] <= step_order[:, None])[None, :, :, None]
    spread = log_decay[:, :, None, :] - log_decay[:, None, :, :]
    decay_table = jnp.where(causal, jnp.exp(jnp.where(causal, spread, 0.0)), 0.0)
    scores = jnp.einsum("stn,sun->stu", c_rows, b_rows, precision=HIGH)
    weights = decay_table * scores[:, :, :, None] * step_size[:, None, :, :]
    within = jnp.einsum("stuh,suhp->sthp", weights, inputs_x, precision=HIGH)
    carried = (
        jnp.einsum("stn,shpn->sthp", c_rows, state_pool, precision=HIGH)
        * jnp.exp(log_decay)[:, :, :, None]
    )
    outputs = within + carried + skip_gain[:, None] * inputs_x
    at_end = (step_order[None, :] == (kept_count - 1)[:, None])[:, :, None]
    end_decay = jnp.sum(jnp.where(at_end, log_decay, 0.0), axis=1)
    before = (step_order[None, :] < kept_count[:, None])[:, :, None]
    gap = end_decay[:, None, :] - log_decay
    select_weight = jnp.where(before, jnp.exp(jnp.where(before, gap, 0.0)), 0.0) * step_size
    chosen = jnp.exp(end_decay)[:, :, None, None] * state_pool + jnp.einsum(
        "suh,suhp,sun->shpn", select_weight, inputs_x, b_rows, precision=HIGH
    )
    series_rows = jnp.arange(series.shape[1], dtype=jnp.int32)
    window = (
        series_rows[None, None, :]
        == kept_count[:, None, None] + jnp.arange(KCONV - 1, dtype=jnp.int32)[None, :, None]
    ).astype(jnp.bfloat16)
    edge_rows = jnp.einsum(
        "sir,src->sic", window, series, preferred_element_type=jnp.float32
    ).astype(jnp.bfloat16)
    return (outputs.reshape(per_dev, draft, inner).astype(jnp.bfloat16), chosen, edge_rows)


def finish(mixed_rows, gate_pre, norm_gain, out_weight):
    gated = mixed_rows.astype(jnp.float32) * jax.nn.silu(gate_pre)
    inner_total = gated.shape[1] * lax.axis_size("mdl")
    squares = lax.psum(jnp.sum(gated * gated, axis=1), "mdl")
    normed = (gated * lax.rsqrt(squares[:, None] / inner_total + EPSILON) * norm_gain).astype(
        jnp.bfloat16
    )
    terms = jnp.dot(
        normed,
        lax.all_gather(out_weight, "req", axis=1, tiled=True),
        preferred_element_type=jnp.float32,
    )
    return lax.psum_scatter(terms, "mdl", scatter_dimension=1, tiled=True).astype(jnp.bfloat16)


def on_device(
    hidden_in,
    z_weight,
    x_weight,
    state_proj,
    step_weight,
    step_bias,
    decay_log,
    skip_gain,
    conv_inner,
    conv_state,
    norm_gain,
    out_weight,
    state_pool,
    conv_pool_inner,
    conv_pool_state,
    owner_dev,
    state_page,
    conv_page,
    accepted,
):
    groups = lax.axis_size("req")
    this_dev = lax.axis_index("req")
    per_dev = state_pool.shape[0]
    draft = hidden_in.shape[0] // per_dev
    slots = WINDOW * CAP
    send_table, gather_table, place_table, conv_of, kept_count = route_tables(
        owner_dev, state_page, conv_page, accepted, groups, per_dev, this_dev
    )
    history = jnp.concatenate([conv_pool_inner[conv_of], conv_pool_state[conv_of]], axis=2)
    kernel = jnp.concatenate([conv_inner, conv_state], axis=1)
    gate_pre, packed, step_raw = project_in(hidden_in, z_weight, x_weight, state_proj, step_weight)
    channels = packed.shape[1]
    payload = jnp.concatenate([packed, step_raw], axis=1)
    total_cols = payload.shape[1]
    outgoing = one_hot_apply(send_table, payload, (slots, draft, total_cols))
    incoming = jnp.concatenate(
        [
            from_behind(outgoing[offset * CAP : (offset + 1) * CAP], "req", offset)
            for offset in range(WINDOW)
        ],
        axis=0,
    )
    owned = one_hot_apply(gather_table, incoming, (per_dev, draft, total_cols))
    mixed_rows, chosen, edge_rows = mix_requests(
        owned[:, :, :channels],
        owned[:, :, channels:],
        history,
        kernel,
        step_bias,
        decay_log,
        skip_gain,
        state_pool,
        kept_count,
    )
    inner_local = mixed_rows.shape[2]
    returning = one_hot_apply(gather_table.T, mixed_rows, (slots, draft, inner_local))
    arrived = jnp.concatenate(
        [
            from_behind(returning[offset * CAP : (offset + 1) * CAP], "req", -offset)
            for offset in range(WINDOW)
        ],
        axis=0,
    )
    home_rows = one_hot_apply(send_table.T, arrived, (per_dev * draft, inner_local))
    mixed = finish(home_rows, gate_pre, norm_gain, out_weight)
    placed = one_hot_apply(place_table, edge_rows, edge_rows.shape)
    inner_cols = conv_pool_inner.shape[2]
    return (mixed, chosen, placed[:, :, :inner_cols], placed[:, :, inner_cols:])


def solution(mesh):
    return jax.shard_map(
        on_device,
        mesh=mesh,
        in_specs=(
            P("req", None),
            P("req", "mdl"),
            P("req", "mdl"),
            P("req", None),
            P("req", "mdl"),
            P("mdl"),
            P("mdl"),
            P("mdl"),
            P(None, "mdl"),
            P(),
            P("mdl"),
            P("mdl", "req"),
            P("req", "mdl", None, None),
            P("req", None, "mdl"),
            P("req", None, None),
            P(),
            P(),
            P(),
            P(),
        ),
        out_specs=(
            P("req", "mdl"),
            P("req", "mdl", None, None),
            P("req", None, "mdl"),
            P("req", None, None),
        ),
        check_vma=False,
    )
```

profile of v0, /device:TPU:1, one launch (start us, length us, event | category | flops | bytes accessed | tf_op | source)
XLA Modules:
  0.0 397.0 jit_solution(18413724058797244592)
XLA Ops:
  14.8 57.0 %all-gather = bf16[64,32,8]{1,2,0:T(8,128)(2,1)S(1)} all-gather(bf16[1,32,8]{1,2,0:T(8,128)(2,1)} %bitcast.102), channel_id=1, replica_groups=mesh['req'=64,'mdl'=8] {'req'}, dimensions={0}, use_global_device_ids=true | all-gather | bytes 33280 | tf_op jit(solution)/shard_map/all_gather | solution.py:54
  74.7 25.1 %all-gather.8.cloned.1.call-done = bf16[2048,256]{1,0:T(8,128)(2,1)} async-done(((bf16[32,256]{1,0:T(8,128)(2,1)}), bf16[2048,256]{1,0:T(8,128)(2,1)}) %all-gather.8.cloned.1.call-update) | async-done | bytes 1048592 | tf_op jit(solution)/shard_map/all_gather | solution.py:53
  99.8 1.5 convolution_convert_fusion.6
  101.3 82.4 %all-gather.6.cloned.1.call-done = bf16[2048,512]{1,0:T(8,128)(2,1)} async-done(((bf16[32,512]{1,0:T(8,128)(2,1)}), bf16[2048,512]{1,0:T(8,128)(2,1)}) %all-gather.6.cloned.1.call-update) | async-done | bytes 2097168 | tf_op jit(solution)/shard_map/all_gather | solution.py:52
  183.8 2.0 convolution_convert_fusion.5
  188.9 2.4 collective-permute-start.1
  191.5 3.1 collective-permute-start.2
  194.8 3.7 collective-permute-start.3
  198.6 2.7 collective-permute-start.4
  201.8 5.9 %collective-permute-start.5 = (bf16[2,16,776]{2,1,0:T(8,128)(2,1)S(1)}, bf16[2,16,776]{2,1,0:T(8,128)(2,1)S(1)}, u32[]{:S(2)}, u32[]{:S(2)}) collective-permute-start(bf16[2,16,776]{2,1,0:T(8,128)(2,1)S(1)} %slice.153), channel_id=1, source_target_pairs={{0,40},{8,48},{16,56},{24,64},{32,72},{40,80},{48,88},{56,96},{64,... | collective-permute-start | bytes 149000 | tf_op jit(solution)/shard_map/ppermute | solution.py:18
  207.7 1.9 collective-permute-start.6
  209.6 4.6 %collective-permute-start.7 = (bf16[2,16,776]{2,1,0:T(8,128)(2,1)S(1)}, bf16[2,16,776]{2,1,0:T(8,128)(2,1)S(1)}, u32[]{:S(2)}, u32[]{:S(2)}) collective-permute-start(bf16[2,16,776]{2,1,0:T(8,128)(2,1)S(1)} %slice.157), channel_id=1, source_target_pairs={{0,56},{8,64},{16,72},{24,80},{32,88},{40,96},{48,104},{56,112},{6... | collective-permute-start | bytes 149000 | tf_op jit(solution)/shard_map/ppermute | solution.py:18
  214.8 2.6 collective-permute-done.7
  224.0 5.8 %convolution_multiply_fusion = f32[8,16,8,64]{3,1,2,0:T(8,128)S(1)} fusion(f32[8,8,64,128]{3,2,1,0:T(8,128)S(1)} %copy-done.1, f32[8,16,8]{1,2,0:T(8,128)} %copy.138, f32[8,16,768]{2,1,0:T(8,128)S(1)} %divide_multiply_fusion), kind=kOutput, calls=%fused_computation.9 | convolution fusion | flops 100728832 | bytes 2428928 | tf_op jit(solution)/shard_map/stn,shpn->sthp/dot_general | solution.py:89
  232.3 1.9 convert_element_type.68
  235.6 1.9 collective-permute-start.9
  237.6 3.3 collective-permute-start.10
  240.9 5.3 %collective-permute-start.11 = (bf16[2,16,512]{2,1,0:T(8,128)(2,1)S(1)}, bf16[2,16,512]{2,1,0:T(8,128)(2,1)S(1)}, u32[]{:S(2)}, u32[]{:S(2)}) collective-permute-start(bf16[2,16,512]{2,1,0:T(8,128)(2,1)S(1)} %bitcast.98), channel_id=1, source_target_pairs={{0,488},{8,496},{16,504},{24,0},{32,8},{40,16},{48,24},{56,32},{64... | collective-permute-start | bytes 98312 | tf_op jit(solution)/shard_map/ppermute | solution.py:18
  246.3 2.9 collective-permute-start.12
  249.2 3.2 collective-permute-start.13
  252.5 2.6 collective-permute-start.14
  255.1 3.8 collective-permute-start.15
  259.0 2.2 collective-permute-done.15
  262.3 1.7 reshape.227
  264.0 3.8 all-gather.10.cloned.1.call-done
  267.8 2.8 multiply_reduce_fusion
  270.6 13.7 %psum.7 = f32[128]{0:T(128)S(1)} all-reduce(f32[128]{0:T(128)S(1)} %get-tuple-element.29), channel_id=1, replica_groups=mesh['req'=64,'mdl'=8] {'mdl'}, use_global_device_ids=true, to_apply=%region_5.6 | all-reduce | flops 128 | bytes 1024 | tf_op jit(solution)/shard_map/psum | solution.py:115
  284.8 66.9 %all-gather.12.cloned.1.call-done = bf16[512,2048]{0,1:T(8,128)(2,1)} async-done(((bf16[512,32]{0,1:T(8,128)(2,1)}), bf16[512,2048]{0,1:T(8,128)(2,1)}) %all-gather.12.cloned.1.call-update) | async-done | bytes 2097168 | tf_op jit(solution)/shard_map/all_gather | solution.py:121
  351.7 3.6 fusion.23
  362.9 5.6 %multiply_add_fusion = f32[8,8,64,128]{3,2,1,0:T(8,128)} fusion(f32[8,8,64,128]{3,2,1,0:T(8,128)S(1)} %copy-done.1, f32[8,8]{1,0:T(8,128)} %exp.41, f32[8,16,8,64]{3,2,1,0:T(8,128)S(1)} %broadcast_multiply_fusion, f32[8,16,768]{2,1,0:T(8,128)S(1)} %divide_multiply_fusion), kind=kOutput, calls=%fused_computation.8 | convolution fusion | flops 101711872 | bytes 4784384 | tf_op jit(solution)/shard_map/suh,suhp,sun->shpn/dot_general | solution.py:98
  368.5 20.3 %reduce-scatter.2.cloned.1.call-done = f32[128,256]{1,0:T(8,128)} async-done(((f32[128,2048]{1,0:T(8,128)}), f32[128,256]{1,0:T(8,128)}) %reduce-scatter.2.cloned.1.call-update) | async-done | bytes 131088 | tf_op jit(solution)/shard_map/reduce_scatter | solution.py:124
  388.9 1.5 convert_element_type.74
  (172 shorter events, 34.5 us)
Async XLA Ops:
  7.2 64.9 %copy-start = (bf16[128,2048]{1,0:T(8,128)(2,1)S(1)}, bf16[128,2048]{1,0:T(8,128)(2,1)}, u32[]{:S(2)}) copy-start(bf16[128,2048]{1,0:T(8,128)(2,1)} %param.19) | copy-start | bytes 1572868
  7.2 92.6 %all-gather.8.cloned.1.call-start = ((), (), s32[]{:S(2)}) async-start(), calls=%async_computation.2 | async-start | bytes 1064960 | tf_op jit(solution)/shard_map/all_gather | solution.py:53
  7.9 175.8 %all-gather.6.cloned.1.call-start = ((), (), s32[]{:S(2)}) async-start(), calls=%async_computation.1 | async-start | bytes 2129920 | tf_op jit(solution)/shard_map/all_gather | solution.py:52
  8.7 259.2 %all-gather.10.cloned.1.call-start = ((), (), s32[]{:S(2)}) async-start(), calls=%async_computation.3 | async-start | bytes 2129920 | tf_op jit(solution)/shard_map/all_gather | solution.py:51
  9.4 342.3 %all-gather.12.cloned.1.call-start = ((), (), s32[]{:S(2)}) async-start(), calls=%async_computation.4 | async-start | bytes 2129920 | tf_op jit(solution)/shard_map/all_gather | solution.py:121
  10.0 378.9 %reduce-scatter.2.cloned.1.call-start = ((), (), s32[]{:S(2)}) async-start(), calls=%async_computation.5 | async-start | bytes 1179648 | tf_op jit(solution)/shard_map/reduce_scatter | solution.py:124
  13.5 170.2 %copy-start.16 = (s32[8]{0:T(128)}, s32[8]{0:T(128)S(1)}, u32[]{:S(2)}) copy-start(s32[8]{0:T(128)S(1)} %get-tuple-element.9) | copy-start | bytes 100
  13.5 170.2 %copy-start.17 = (s32[8]{0:T(128)}, s32[8]{0:T(128)S(1)}, u32[]{:S(2)}) copy-start(s32[8]{0:T(128)S(1)} %get-tuple-element.8) | copy-start | bytes 100
  13.5 204.3 %copy-start.13 = (s32[8]{0:T(128)}, s32[8]{0:T(128)S(1)}, u32[]{:S(2)}) copy-start(s32[8]{0:T(128)S(1)} %get-tuple-element.10) | copy-start | bytes 100
  74.7 111.4 %copy-start.11 = (s32[8]{0:T(128)}, s32[8]{0:T(128)S(1)}, u32[]{:S(2)}) copy-start(s32[8]{0:T(128)S(1)} %dynamic-slice_reduce_fusion) | copy-start | bytes 100
  101.3 86.1 %copy-start.3 = (bf16[8,3,256]{2,0,1:T(8,128)(2,1)S(1)}, bf16[8,3,256]{2,0,1:T(8,128)(2,1)}, u32[]{:S(2)}) copy-start(bf16[8,3,256]{2,0,1:T(8,128)(2,1)} %param.33) | copy-start | bytes 36868
  101.3 86.7 %copy-start.2 = (bf16[8,3,512]{2,0,1:T(8,128)(2,1)S(1)}, bf16[8,3,512]{2,0,1:T(8,128)(2,1)}, u32[]{:S(2)}) copy-start(bf16[8,3,512]{2,0,1:T(8,128)(2,1)} %param.32) | copy-start | bytes 73732
  186.8 15.0 %collective-permute-start = (bf16[2,16,776]{2,1,0:T(8,128)(2,1)S(1)}, bf16[2,16,776]{2,1,0:T(8,128)(2,1)S(1)}, u32[]{:S(2)}, u32[]{:S(2)}) collective-permute-start(bf16[2,16,776]{2,1,0:T(8,128)(2,1)S(1)} %slice.143), channel_id=1, source_target_pairs={{0,0},{8,8},{16,16},{24,24},{32,32},{40,40},{48,48},{56,56},{64,64... | collective-permute-start | bytes 149000 | tf_op jit(solution)/shard_map/ppermute | solution.py:18
  188.0 32.2 %copy-start.8 = (bf16[8,3,256]{2,1,0:T(4,128)(2,1)}, bf16[8,3,256]{2,1,0:T(4,128)(2,1)S(1)}, u32[]{:S(2)}) copy-start(bf16[8,3,256]{2,1,0:T(4,128)(2,1)S(1)} %copy.130) | copy-start | bytes 36868
  188.7 29.9 %copy-start.14 = (f32[8]{0:T(128)S(1)}, f32[8]{0:T(128)}, u32[]{:S(2)}) copy-start(f32[8]{0:T(128)} %param.24) | copy-start | bytes 100
  188.7 31.5 %copy-start.6 = (bf16[8,3,512]{2,1,0:T(4,128)(2,1)}, bf16[8,3,512]{2,1,0:T(4,128)(2,1)S(1)}, u32[]{:S(2)}) copy-start(bf16[8,3,512]{2,1,0:T(4,128)(2,1)S(1)} %copy.129) | copy-start | bytes 73732
  188.9 18.8 %collective-permute-start.1 = (bf16[2,16,776]{2,1,0:T(8,128)(2,1)S(1)}, bf16[2,16,776]{2,1,0:T(8,128)(2,1)S(1)}, u32[]{:S(2)}, u32[]{:S(2)}) collective-permute-start(bf16[2,16,776]{2,1,0:T(8,128)(2,1)S(1)} %slice.145), channel_id=1, source_target_pairs={{0,8},{8,16},{16,24},{24,32},{32,40},{40,48},{48,56},{56,64},{64,7... | collective-permute-start | bytes 149000 | tf_op jit(solution)/shard_map/ppermute | solution.py:18
  191.5 18.1 %collective-permute-start.2 = (bf16[2,16,776]{2,1,0:T(8,128)(2,1)S(1)}, bf16[2,16,776]{2,1,0:T(8,128)(2,1)S(1)}, u32[]{:S(2)}, u32[]{:S(2)}) collective-permute-start(bf16[2,16,776]{2,1,0:T(8,128)(2,1)S(1)} %slice.147), channel_id=1, source_target_pairs={{0,16},{8,24},{16,32},{24,40},{32,48},{40,56},{48,64},{56,72},{64,... | collective-permute-start | bytes 149000 | tf_op jit(solution)/shard_map/ppermute | solution.py:18
  194.8 19.5 %collective-permute-start.3 = (bf16[2,16,776]{2,1,0:T(8,128)(2,1)S(1)}, bf16[2,16,776]{2,1,0:T(8,128)(2,1)S(1)}, u32[]{:S(2)}, u32[]{:S(2)}) collective-permute-start(bf16[2,16,776]{2,1,0:T(8,128)(2,1)S(1)} %slice.149), channel_id=1, source_target_pairs={{0,24},{8,32},{16,40},{24,48},{32,56},{40,64},{48,72},{56,80},{64,... | collective-permute-start | bytes 149000 | tf_op jit(solution)/shard_map/ppermute | solution.py:18
  198.6 15.7 %collective-permute-start.4 = (bf16[2,16,776]{2,1,0:T(8,128)(2,1)S(1)}, bf16[2,16,776]{2,1,0:T(8,128)(2,1)S(1)}, u32[]{:S(2)}, u32[]{:S(2)}) collective-permute-start(bf16[2,16,776]{2,1,0:T(8,128)(2,1)S(1)} %slice.151), channel_id=1, source_target_pairs={{0,32},{8,40},{16,48},{24,56},{32,64},{40,72},{48,80},{56,88},{64,... | collective-permute-start | bytes 149000 | tf_op jit(solution)/shard_map/ppermute | solution.py:18
  201.8 12.6 %collective-permute-start.5 = (bf16[2,16,776]{2,1,0:T(8,128)(2,1)S(1)}, bf16[2,16,776]{2,1,0:T(8,128)(2,1)S(1)}, u32[]{:S(2)}, u32[]{:S(2)}) collective-permute-start(bf16[2,16,776]{2,1,0:T(8,128)(2,1)S(1)} %slice.153), channel_id=1, source_target_pairs={{0,40},{8,48},{16,56},{24,64},{32,72},{40,80},{48,88},{56,96},{64,... | collective-permute-start | bytes 149000 | tf_op jit(solution)/shard_map/ppermute | solution.py:18
  207.7 7.1 %collective-permute-start.6 = (bf16[2,16,776]{2,1,0:T(8,128)(2,1)S(1)}, bf16[2,16,776]{2,1,0:T(8,128)(2,1)S(1)}, u32[]{:S(2)}, u32[]{:S(2)}) collective-permute-start(bf16[2,16,776]{2,1,0:T(8,128)(2,1)S(1)} %slice.155), channel_id=1, source_target_pairs={{0,48},{8,56},{16,64},{24,72},{32,80},{40,88},{48,96},{56,104},{64... | collective-permute-start | bytes 149000 | tf_op jit(solution)/shard_map/ppermute | solution.py:18
  209.6 7.8 %collective-permute-start.7 = (bf16[2,16,776]{2,1,0:T(8,128)(2,1)S(1)}, bf16[2,16,776]{2,1,0:T(8,128)(2,1)S(1)}, u32[]{:S(2)}, u32[]{:S(2)}) collective-permute-start(bf16[2,16,776]{2,1,0:T(8,128)(2,1)S(1)} %slice.157), channel_id=1, source_target_pairs={{0,56},{8,64},{16,72},{24,80},{32,88},{40,96},{48,104},{56,112},{6... | collective-permute-start | bytes 149000 | tf_op jit(solution)/shard_map/ppermute | solution.py:18
  231.5 29.9 %copy-start.12 = (s32[8]{0:T(128)S(1)}, s32[8]{0:T(128)}, u32[]{:S(2)}) copy-start(s32[8]{0:T(128)} %copy-done.11) | copy-start | bytes 100
  235.6 13.6 %collective-permute-start.8 = (bf16[2,16,512]{2,1,0:T(8,128)(2,1)S(1)}, bf16[2,16,512]{2,1,0:T(8,128)(2,1)S(1)}, u32[]{:S(2)}, u32[]{:S(2)}) collective-permute-start(bf16[2,16,512]{2,1,0:T(8,128)(2,1)S(1)} %bitcast.101), channel_id=1, source_target_pairs={{0,0},{8,8},{16,16},{24,24},{32,32},{40,40},{48,48},{56,56},{64,64... | collective-permute-start | bytes 98312 | tf_op jit(solution)/shard_map/ppermute | solution.py:18
  235.6 16.9 %collective-permute-start.9 = (bf16[2,16,512]{2,1,0:T(8,128)(2,1)S(1)}, bf16[2,16,512]{2,1,0:T(8,128)(2,1)S(1)}, u32[]{:S(2)}, u32[]{:S(2)}) collective-permute-start(bf16[2,16,512]{2,1,0:T(8,128)(2,1)S(1)} %bitcast.100), channel_id=1, source_target_pairs={{0,504},{8,0},{16,8},{24,16},{32,24},{40,32},{48,40},{56,48},{64,5... | collective-permute-start | bytes 98312 | tf_op jit(solution)/shard_map/ppermute | solution.py:18
  237.6 17.5 %collective-permute-start.10 = (bf16[2,16,512]{2,1,0:T(8,128)(2,1)S(1)}, bf16[2,16,512]{2,1,0:T(8,128)(2,1)S(1)}, u32[]{:S(2)}, u32[]{:S(2)}) collective-permute-start(bf16[2,16,512]{2,1,0:T(8,128)(2,1)S(1)} %bitcast.99), channel_id=1, source_target_pairs={{0,496},{8,504},{16,0},{24,8},{32,16},{40,24},{48,32},{56,40},{64,... | collective-permute-start | bytes 98312 | tf_op jit(solution)/shard_map/ppermute | solution.py:18
  240.9 18.0 %collective-permute-start.11 = (bf16[2,16,512]{2,1,0:T(8,128)(2,1)S(1)}, bf16[2,16,512]{2,1,0:T(8,128)(2,1)S(1)}, u32[]{:S(2)}, u32[]{:S(2)}) collective-permute-start(bf16[2,16,512]{2,1,0:T(8,128)(2,1)S(1)} %bitcast.98), channel_id=1, source_target_pairs={{0,488},{8,496},{16,504},{24,0},{32,8},{40,16},{48,24},{56,32},{64... | collective-permute-start | bytes 98312 | tf_op jit(solution)/shard_map/ppermute | solution.py:18
  246.3 12.7 %collective-permute-start.12 = (bf16[2,16,512]{2,1,0:T(8,128)(2,1)S(1)}, bf16[2,16,512]{2,1,0:T(8,128)(2,1)S(1)}, u32[]{:S(2)}, u32[]{:S(2)}) collective-permute-start(bf16[2,16,512]{2,1,0:T(8,128)(2,1)S(1)} %bitcast.97), channel_id=1, source_target_pairs={{0,480},{8,488},{16,496},{24,504},{32,0},{40,8},{48,16},{56,24},{6... | collective-permute-start | bytes 98312 | tf_op jit(solution)/shard_map/ppermute | solution.py:18
  249.2 9.8 %collective-permute-start.13 = (bf16[2,16,512]{2,1,0:T(8,128)(2,1)S(1)}, bf16[2,16,512]{2,1,0:T(8,128)(2,1)S(1)}, u32[]{:S(2)}, u32[]{:S(2)}) collective-permute-start(bf16[2,16,512]{2,1,0:T(8,128)(2,1)S(1)} %bitcast.96), channel_id=1, source_target_pairs={{0,472},{8,480},{16,488},{24,496},{32,504},{40,0},{48,8},{56,16},{... | collective-permute-start | bytes 98312 | tf_op jit(solution)/shard_map/ppermute | solution.py:18
  252.5 6.5 %collective-permute-start.14 = (bf16[2,16,512]{2,1,0:T(8,128)(2,1)S(1)}, bf16[2,16,512]{2,1,0:T(8,128)(2,1)S(1)}, u32[]{:S(2)}, u32[]{:S(2)}) collective-permute-start(bf16[2,16,512]{2,1,0:T(8,128)(2,1)S(1)} %bitcast.95), channel_id=1, source_target_pairs={{0,464},{8,472},{16,480},{24,488},{32,496},{40,504},{48,0},{56,8},... | collective-permute-start | bytes 98312 | tf_op jit(solution)/shard_map/ppermute | solution.py:18
  255.1 6.1 %collective-permute-start.15 = (bf16[2,16,512]{2,1,0:T(8,128)(2,1)S(1)}, bf16[2,16,512]{2,1,0:T(8,128)(2,1)S(1)}, u32[]{:S(2)}, u32[]{:S(2)}) collective-permute-start(bf16[2,16,512]{2,1,0:T(8,128)(2,1)S(1)} %bitcast.94), channel_id=1, source_target_pairs={{0,456},{8,464},{16,472},{24,480},{32,488},{40,496},{48,504},{56,0... | collective-permute-start | bytes 98312 | tf_op jit(solution)/shard_map/ppermute | solution.py:18
  (11 other events, 55.2 us)
Sparse Core Ops, SparseCore 0:
  11.4 88.3 all-gather.7
  103.1 80.5 all-gather.5
  187.1 80.6 all-gather.9
  271.0 80.5 all-gather.11
  355.4 33.4 reduce-scatter.1
where the time goes:
time: 402 us; the launch traced here: 397 us
  waiting for transfers between devices  206 us (51%)
  blocking collectives  70.7 us (18%)
  starting transfers between devices  47.6 us (12%)
  matrix products  27.8 us (7%)
  local copies, waits for them, and re-layouts  19.2 us (5%)
  between operations  14.7 us (4%)
  other arithmetic  10.6 us (3%)
    all_gather x1, waiting for transfers between devices, project_in(): lax.all_gather(x_weight, 'req', axis=0, tiled=True)  82.4 us
    all_gather x1, waiting for transfers between devices, finish(): lax.all_gather(out_weight, 'req', axis=1, tiled=True)  66.9 us
    all_gather x1, blocking collectives, project_in(): lax.all_gather(step_weight, 'req', axis=0, tiled=True)  57 us
    ppermute x16, starting transfers between devices, from_behind(): return lax.ppermute(value, axis, pairs)  47.4 us
    all_gather x1, waiting for transfers between devices, project_in(): lax.all_gather(state_proj, 'req', axis=0, tiled=True)  25.1 us
    reduce_scatter x1, waiting for transfers between devices, finish(): lax.psum_scatter(terms, 'mdl', scatter_dimension=1, tiled=True)  20.3 us
    psum x1, blocking collectives, finish(): squares = lax.psum(jnp.sum(gated * gated, axis=1), 'mdl')  13.7 us
  transfers between devices with their start and end apart: 21, of which 8 were waited for; matrix products, arithmetic and copies ran while one was open for 13% of the time, Pallas kernels for 0%

commit v1 on v0

v1 whole, which is shorter than its diff:
```python
import functools

import jax
import jax.numpy as jnp
from jax import lax
from jax.experimental import pallas as pl
from jax.experimental.pallas import tpu as pltpu
from jax.sharding import PartitionSpec as P

KCONV = 4
CAP = 2
WINDOW = 8
SLOTS = WINDOW * CAP
XN = 4
HIGH = lax.Precision.HIGHEST
EPSILON = 1e-05
MESH = pl.DeviceIdType.MESH
NT = (((1,), (1,)), ((), ()))


def route_tables(owner_dev, state_page, conv_page, accepted, groups, per_dev, this_dev):
    owner_grid = owner_dev.reshape(groups, per_dev)
    home_grid = jnp.arange(groups, dtype=jnp.int32)[:, None]
    offset_grid = (owner_grid - home_grid + groups) % groups
    positions = jnp.arange(per_dev, dtype=jnp.int32)
    earlier = positions[None, :] < positions[:, None]
    pair_rank = jnp.sum((owner_grid[:, :, None] == owner_grid[:, None, :]) & earlier[None], axis=2)
    slot_grid = offset_grid * CAP + pair_rank
    slot_of = lax.dynamic_slice_in_dim(slot_grid, this_dev, 1, 0)[0]
    slot_ids = jnp.arange(SLOTS, dtype=jnp.int32)
    source_of = jnp.sum(
        jnp.where(slot_ids[:, None] == slot_of[None, :], positions[None, :], 0), axis=1
    )
    arrive_at = slot_grid.reshape(-1)
    match = (owner_dev[None, :] == this_dev) & (state_page[None, :] == positions[:, None])
    pick_from = jnp.sum(jnp.where(match, arrive_at[None, :], 0), axis=1)
    conv_of = jnp.sum(jnp.where(match, conv_page[None, :], 0), axis=1)
    kept_count = jnp.sum(jnp.where(match, accepted[None, :], 0), axis=1)
    page_of = jnp.sum(
        jnp.where(slot_ids[:, None] == pick_from[None, :], positions[None, :], 0), axis=1
    )
    return slot_of, source_of, pick_from, page_of, conv_of, kept_count


def greet(peers):
    barrier = pltpu.get_barrier_semaphore()
    for peer in peers:
        pl.semaphore_signal(barrier, inc=1, device_id=peer, device_id_type=MESH)
    pl.semaphore_wait(barrier, len(peers))


class Copies:
    def __init__(self, send_sem, recv_sem):
        self.send_sem, self.recv_sem = send_sem, recv_sem
        self.keys, self.started = {}, []

    def key(self, name):
        return self.keys.setdefault(name, len(self.keys))

    def send(self, name, src, dst, peer):
        k = self.key(name)
        copy = pltpu.make_async_remote_copy(
            src_ref=src,
            dst_ref=dst,
            send_sem=self.send_sem.at[k],
            recv_sem=self.recv_sem.at[k],
            device_id=peer,
            device_id_type=MESH,
        )
        copy.start()
        self.started.append(copy)

    def arrive(self, name, where, peer):
        k = self.key(name)
        pltpu.make_async_remote_copy(
            src_ref=where,
            dst_ref=where,
            send_sem=self.send_sem.at[k],
            recv_sem=self.recv_sem.at[k],
            device_id=peer,
            device_id_type=MESH,
        ).wait_recv()

    def finish(self):
        for copy in self.started:
            copy.wait_send()


def gather_kernel(
    groups,
    mdl_size,
    source_of,
    pick_from,
    hidden,
    shard,
    full,
    rows_full,
    outgoing,
    incoming,
    owned,
    send_sem,
    recv_sem,
    own_sem,
):
    zn = groups // (2 * XN)
    me = lax.axis_index("req")
    col = lax.axis_index("mdl")
    core = me % 2
    x = (me // 2) % XN
    z = me // (2 * XN)
    width = hidden.shape[2] // mdl_size

    def at(zz, xx, cc):
        return {"req": ((zz + zn) % zn * XN + (xx + XN) % XN) * 2 + cc}

    def zi(v):
        return (v + zn) % zn

    def xi(v):
        return (v + XN) % XN

    sibling = {"req": me + 1 - 2 * core}
    up, down = at(z + 1, x, core), at(z - 1, x, core)
    xs = [at(z, x + d, core) for d in range(1, XN)]
    ahead = [{"req": (me + o) % groups} for o in range(1, WINDOW)]
    behind = [{"req": (me - o + groups) % groups} for o in range(1, WINDOW)]
    across = [{"mdl": (col + k) % mdl_size} for k in range(1, mdl_size)]
    greet([sibling, up, down] + xs + ahead + behind + across)

    copies = Copies(send_sem, recv_sem)
    half_up = zn // 2
    half_down = (zn - 1) // 2
    split_z = zn % 2 == 0
    hx = XN // 2

    own = pltpu.make_async_copy(shard, full.at[z, x, core], own_sem.at[0])
    own.start()
    for d in range(1, XN):
        copies.send(("ax", d), shard.at[0], full.at[z, x, core, 0], xs[d - 1])
    copies.send(("bu", 1), shard.at[1], full.at[z, x, core, 1], up)
    copies.send(("bd", 1), shard.at[1], full.at[z, x, core, 1], down)

    for s in range(SLOTS):
        outgoing[s] = hidden[source_of[s], :, pl.ds(pl.multiple_of(col * width, width), width)]
    for o in range(1, WINDOW):
        part = pl.ds(o * CAP, CAP)
        copies.send(("h", o), outgoing.at[part], incoming.at[part], ahead[o - 1])
    incoming[0:CAP] = outgoing[0:CAP]

    for s in range(1, half_up + 1):
        piece = full.at[zi(z - s), x, core, 1]
        copies.arrive(("bu", s), piece, up)
        if s < half_up:
            copies.send(("bu", s + 1), piece, piece, up)
        if s <= half_down:
            piece = full.at[zi(z + s), x, core, 1]
            copies.arrive(("bd", s), piece, up)
            if s < half_down:
                copies.send(("bd", s + 1), piece, piece, down)
        if s == 1:
            own.wait()
            for d in range(1, XN):
                copies.arrive(("ax", d), full.at[z, xi(x - d), core, 0], up)
            block = full.at[z, :, core, 0]
            copies.send(("au", 1), block, block, up)
            copies.send(("ad", 1), block, block, down)
            copies.send(("sa", 0), block, block, sibling)
    line = full.at[:, x, core, 1]
    copies.send(("bx", 1), line, line, at(z, x + 1, core))
    copies.send(("bx", 3), line, line, at(z, x - 1, core))
    copies.send(("sb", 0), line, line, sibling)

    for o in range(1, WINDOW):
        copies.arrive(("h", o), incoming.at[pl.ds(o * CAP, CAP)], up)
    for p in range(hidden.shape[0]):
        owned[p] = incoming[pick_from[p]]
    keep = pltpu.make_async_copy(owned, rows_full.at[col], own_sem.at[1])
    keep.start()
    for k in range(1, mdl_size):
        copies.send(("y", k), owned, rows_full.at[col], across[k - 1])

    def forward_x():
        back, front = full.at[:, xi(x - 1), core, 1], full.at[:, xi(x + 1), core, 1]
        copies.arrive(("bx", 1), back, up)
        copies.arrive(("bx", 3), front, up)
        low, high = pl.ds(0, half_up), pl.ds(half_up, zn - half_up)
        a = full.at[low, xi(x - 1), core, 1]
        b = full.at[high, xi(x + 1), core, 1]
        copies.send(("bx", 2), a, a, at(z, x + 1, core))
        copies.send(("bx", 4), b, b, at(z, x - 1, core))
        copies.send(("sb", 1), back, back, sibling)
        copies.send(("sb", 3), front, front, sibling)

    for s in range(1, half_up + 1):
        last = split_z and s == half_up
        xu = pl.ds(0, hx) if last else pl.ds(0, XN)
        xd = pl.ds(hx, XN - hx) if last else pl.ds(0, XN)
        bu = full.at[zi(z - s), xu, core, 0]
        bd = full.at[zi(z + s), xd, core, 0]
        copies.arrive(("au", s), bu, up)
        if s < half_up:
            nu = pl.ds(0, hx) if split_z and s + 1 == half_up else xu
            piece = full.at[zi(z - s), nu, core, 0]
            copies.send(("au", s + 1), piece, piece, up)
        copies.arrive(("ad", s), bd, up)
        if s < half_up:
            nd = pl.ds(hx, XN - hx) if split_z and s + 1 == half_up else xd
            piece = full.at[zi(z + s), nd, core, 0]
            copies.send(("ad", s + 1), piece, piece, down)
        copies.send(("sau", s), bu, bu, sibling)
        copies.send(("sad", s), bd, bd, sibling)
        if s == half_up - 1:
            forward_x()

    far = xi(x + 2)
    low, high = pl.ds(0, half_up), pl.ds(half_up, zn - half_up)
    copies.arrive(("bx", 2), full.at[low, far, core, 1], up)
    copies.arrive(("bx", 4), full.at[high, far, core, 1], up)
    rest = full.at[:, far, core, 1]
    copies.send(("sb", 2), rest, rest, sibling)

    other = 1 - core
    copies.arrive(("sa", 0), full.at[z, :, other, 0], up)
    for j in range(XN):
        copies.arrive(("sb", j), full.at[:, xi(x - j), other, 1], up)
    for s in range(1, half_up + 1):
        last = split_z and s == half_up
        xu = pl.ds(0, hx) if last else pl.ds(0, XN)
        xd = pl.ds(hx, XN - hx) if last else pl.ds(0, XN)
        copies.arrive(("sau", s), full.at[zi(z - s), xu, other, 0], up)
        copies.arrive(("sad", s), full.at[zi(z + s), xd, other, 0], up)
    for k in range(1, mdl_size):
        copies.arrive(("y", k), rows_full.at[(col - k + mdl_size) % mdl_size], up)
    keep.wait()
    copies.finish()


def gather(source_of, pick_from, hidden, shard, groups, mdl_size):
    per_dev, draft, depth = hidden.shape
    zn = groups // (2 * XN)
    width = depth // mdl_size
    count = 96
    return pl.pallas_call(
        functools.partial(gather_kernel, groups, mdl_size),
        out_shape=(
            jax.ShapeDtypeStruct((zn, XN, 2) + shard.shape, shard.dtype),
            jax.ShapeDtypeStruct((mdl_size, per_dev, draft, width), hidden.dtype),
        ),
        in_specs=[
            pl.BlockSpec(memory_space=pltpu.SMEM),
            pl.BlockSpec(memory_space=pltpu.SMEM),
            pl.BlockSpec(memory_space=pltpu.VMEM),
            pl.BlockSpec(memory_space=pl.ANY),
        ],
        out_specs=(
            pl.BlockSpec(memory_space=pl.ANY),
            pl.BlockSpec(memory_space=pl.ANY),
        ),
        scratch_shapes=[
            pltpu.VMEM((SLOTS, draft, width), hidden.dtype),
            pltpu.VMEM((SLOTS, draft, width), hidden.dtype),
            pltpu.VMEM((per_dev, draft, width), hidden.dtype),
            pltpu.SemaphoreType.DMA((count,)),
            pltpu.SemaphoreType.DMA((count,)),
            pltpu.SemaphoreType.DMA((2,)),
        ],
        compiler_params=pltpu.CompilerParams(collective_id=0, has_side_effects=True),
        name="gather_rows_and_weights",
    )(source_of, pick_from, hidden, shard)


def dot(a, b, precision=None):
    return jnp.dot(a, b, preferred_element_type=jnp.float32, precision=precision)


def dot_nt(a, b, precision=None):
    return lax.dot_general(a, b, NT, preferred_element_type=jnp.float32, precision=precision)


def mix_kernel(
    dims,
    conv_of,
    kept,
    step_bias,
    decay_log,
    skip_gain,
    rows_full,
    weights,
    conv_inner,
    conv_state,
    norm_gain,
    state_pool,
    hist_inner,
    hist_state,
    terms,
    squares,
    new_states,
    edge_inner,
    edge_state,
    acc,
    out_t,
    series_x,
    series_s,
    hist_x,
    hist_s,
    edge_x,
    edge_s,
    carried,
):
    per_dev, draft, heads, hdim, nstate, inner, columns = dims
    step = pl.program_id(0)
    depth = weights.shape[0]
    tokens = per_dev * draft
    wide = 2 * inner + 2 * nstate + 128
    blk = rows_full[...].reshape(tokens, depth)
    part = dot(blk, weights[:, :wide])
    out_t[pl.ds(pl.multiple_of(step * depth, depth), depth), :] = weights[:, wide:]

    @pl.when(step == 0)
    def _():
        acc[...] = part

    @pl.when(step > 0)
    def _():
        acc[...] += part

    @pl.when(step == pl.num_programs(0) - 1)
    def _():
        f32, bf16 = jnp.float32, jnp.bfloat16
        hist_x[...] = hist_inner[...].astype(f32)
        hist_s[...] = hist_state[...].astype(f32)
        x_raw = acc[:, inner : 2 * inner].astype(bf16).astype(f32)
        s_raw = acc[:, 2 * inner : 2 * inner + 2 * nstate].astype(bf16).astype(f32)
        series_x[:, 8:, :] = x_raw.reshape(per_dev, draft, inner)
        series_s[:, 8:, :] = s_raw.reshape(per_dev, draft, 2 * nstate)
        lead = 8 - (KCONV - 1)
        for p in range(per_dev):
            for j in range(KCONV - 1):
                series_x[p, lead + j : lead + j + 1, :] = hist_x[j, pl.ds(conv_of[p], 1), :]
                series_s[p, lead + j : lead + j + 1, :] = hist_s[j, pl.ds(conv_of[p], 1), :]
        for p in range(per_dev):
            for j in range(KCONV - 1):
                edge_x[j, pl.ds(conv_of[p], 1), :] = series_x[p, pl.ds(lead + kept[p] + j, 1), :]
                edge_s[j, pl.ds(conv_of[p], 1), :] = series_s[p, pl.ds(lead + kept[p] + j, 1), :]
        edge_inner[...] = edge_x[...].astype(bf16)
        edge_state[...] = edge_s[...].astype(bf16)

        def conv(series, taps):
            total = taps[0:1, :] * series[:, lead : lead + draft, :]
            for k in range(1, KCONV):
                total = total + taps[k : k + 1, :] * series[:, lead + k : lead + k + draft, :]
            return jax.nn.silu(total).reshape(tokens, total.shape[2])

        active = conv(series_x, conv_inner)
        maps = conv(series_s, conv_state)
        b_rows, c_rows = maps[:, :nstate], maps[:, nstate:]

        lane = lax.broadcasted_iota(jnp.int32, (1, 128), 1)
        bias_row = jnp.zeros((1, 128), f32)
        rate_row = jnp.zeros((1, 128), f32)
        for h in range(heads):
            bias_row = jnp.where(lane == h, step_bias[h], bias_row)
            rate_row = jnp.where(lane == h, decay_log[h], rate_row)
        rate_row = jnp.exp(rate_row)
        step_raw = acc[:, 2 * inner + 2 * nstate : wide].astype(bf16).astype(f32)
        size = jax.nn.softplus(step_raw + bias_row)
        rows_i = lax.broadcasted_iota(jnp.int32, (tokens, tokens), 0)
        cols_i = lax.broadcasted_iota(jnp.int32, (tokens, tokens), 1)
        causal = (rows_i // draft == cols_i // draft) & (cols_i <= rows_i)
        decay = dot(causal.astype(f32), -size * rate_row, HIGH)
        decay_t, size_t = decay.T, size.T
        scores = dot_nt(c_rows, b_rows, HIGH)

        end_at = jnp.zeros((tokens, tokens), jnp.int32)
        for p in range(per_dev):
            end_at = jnp.where(rows_i // draft == p, p * draft + kept[p] - 1, end_at)
        end_decay = dot((cols_i == end_at).astype(f32), decay, HIGH)
        before = rows_i <= end_at
        chosen_w = jnp.where(before, jnp.exp(jnp.where(before, end_decay - decay, 0.0)), 0.0) * size
        grown = jnp.exp(decay)
        end_grown = jnp.exp(end_decay)

        b_low = b_rows.astype(bf16)
        c_low = c_rows.astype(bf16)
        for p in range(per_dev):
            start = state_pool[p].reshape(inner, nstate)
            carried[p * draft : (p + 1) * draft, :] = dot_nt(
                c_low[p * draft : (p + 1) * draft, :], start.astype(bf16)
            )

        left = lax.broadcasted_iota(jnp.int32, (tokens, 128), 1) < hdim

        def spread(table, j):
            return jnp.where(left, table[:, 2 * j : 2 * j + 1], table[:, 2 * j + 1 : 2 * j + 2])

        total = jnp.zeros((tokens, 128), f32)
        gated_cols = []
        picked_t = []
        for j in range(heads // 2):
            cols = slice(j * 128, (j + 1) * 128)
            x_pair = active[:, cols]
            x_low = x_pair.astype(bf16)
            halves = []
            for h in (2 * j, 2 * j + 1):
                gap = decay[:, h : h + 1] - decay_t[h : h + 1, :]
                weight = jnp.exp(jnp.where(causal, gap, -1e30)) * scores * size_t[h : h + 1, :]
                halves.append(dot(weight.astype(bf16), x_low))
            skip = jnp.where(left, skip_gain[2 * j], skip_gain[2 * j + 1])
            y = (
                jnp.where(left, halves[0], halves[1])
                + carried[:, cols] * spread(grown, j)
                + skip * x_pair
            )
            gate = jax.nn.silu(acc[:, cols])
            gated = y.astype(bf16).astype(f32) * gate
            total = total + gated * gated
            gated_cols.append((gated * norm_gain[0:1, cols]).astype(bf16))
            picked_t.append((x_pair * spread(chosen_w, j)).T.astype(bf16))
        gated_low = jnp.concatenate(gated_cols, axis=1)
        squares[...] = dot_nt(jnp.ones((8, 128), f32), total, HIGH)
        piece = out_t.shape[0] // terms.shape[0]
        for m in range(terms.shape[0]):
            terms[m] = dot_nt(gated_low, out_t[m * piece : (m + 1) * piece, :]).astype(bf16)

        picked = jnp.concatenate(picked_t, axis=0)
        row_of = lax.broadcasted_iota(jnp.int32, (tokens, nstate), 0) // draft
        for p in range(per_dev):
            masked = jnp.where(row_of == p, b_low, jnp.zeros_like(b_low))
            added = dot(picked, masked)
            for h in range(heads):
                factor = end_grown[p * draft : p * draft + 1, h : h + 1]
                new_states[p, h] = factor * state_pool[p, h] + added[h * hdim : (h + 1) * hdim, :]


def mix(
    conv_of,
    kept,
    step_bias,
    decay_log,
    skip_gain,
    rows_full,
    weights,
    conv_inner,
    conv_state,
    norm_gain,
    state_pool,
    hist_inner,
    hist_state,
):
    mdl_size, per_dev, draft, width = rows_full.shape
    _, heads, hdim, nstate = state_pool.shape
    depth, packed = weights.shape
    inner = heads * hdim
    tokens = per_dev * draft
    columns = depth
    smem = pl.BlockSpec(memory_space=pltpu.SMEM)

    def whole(a):
        return pl.BlockSpec(
            a.shape, lambda k: (0,) * len(a.shape), pipeline_mode=pl.Buffered(1)
        )

    out_shape = (
        jax.ShapeDtypeStruct((mdl_size, tokens, columns // mdl_size), jnp.bfloat16),
        jax.ShapeDtypeStruct((8, tokens), jnp.float32),
        jax.ShapeDtypeStruct(state_pool.shape, state_pool.dtype),
        jax.ShapeDtypeStruct(hist_inner.shape, hist_inner.dtype),
        jax.ShapeDtypeStruct(hist_state.shape, hist_state.dtype),
    )
    f32 = jnp.float32
    return pl.pallas_call(
        functools.partial(mix_kernel, (per_dev, draft, heads, hdim, nstate, inner, columns)),
        grid=(mdl_size,),
        out_shape=out_shape,
        in_specs=[smem] * 5
        + [
            pl.BlockSpec((None, per_dev, draft, width), lambda k: (k, 0, 0, 0)),
            pl.BlockSpec((width, packed), lambda k: (k, 0)),
        ]
        + [
            whole(a)
            for a in (conv_inner, conv_state, norm_gain, state_pool, hist_inner, hist_state)
        ],
        out_specs=tuple(whole(o) for o in out_shape),
        scratch_shapes=[
            pltpu.VMEM((tokens, 2 * inner + 2 * nstate + 128), f32),
            pltpu.VMEM((depth, inner), jnp.bfloat16),
            pltpu.VMEM((per_dev, draft + 8, inner), f32),
            pltpu.VMEM((per_dev, draft + 8, 2 * nstate), f32),
            pltpu.VMEM((KCONV - 1, per_dev, inner), f32),
            pltpu.VMEM((KCONV - 1, per_dev, 2 * nstate), f32),
            pltpu.VMEM((KCONV - 1, per_dev, inner), f32),
            pltpu.VMEM((KCONV - 1, per_dev, 2 * nstate), f32),
            pltpu.VMEM((tokens, inner), f32),
        ],
        compiler_params=pltpu.CompilerParams(vmem_limit_bytes=40 << 20),
        name="project_and_mix",
    )(
        conv_of,
        kept,
        step_bias,
        decay_log,
        skip_gain,
        rows_full,
        weights,
        conv_inner,
        conv_state,
        norm_gain,
        state_pool,
        hist_inner,
        hist_state,
    )


def return_kernel(
    groups,
    mdl_size,
    page_of,
    slot_of,
    terms,
    squares,
    mixed,
    parts,
    square_parts,
    result,
    outgoing,
    incoming,
    send_sem,
    recv_sem,
):
    me = lax.axis_index("req")
    col = lax.axis_index("mdl")
    per_dev, draft, columns = mixed.shape
    tokens = per_dev * draft
    ahead = [{"req": (me + o) % groups} for o in range(1, WINDOW)]
    behind = [{"req": (me - o + groups) % groups} for o in range(1, WINDOW)]
    across = [{"mdl": (col + k) % mdl_size} for k in range(1, mdl_size)]
    greet(ahead + behind + across)
    copies = Copies(send_sem, recv_sem)
    for k in range(1, mdl_size):
        copies.send(("s", k), squares, square_parts.at[k], across[k - 1])
    for k in sorted(range(1, mdl_size), key=lambda k: -min(k, mdl_size - k)):
        copies.send(("t", k), terms.at[(col + k) % mdl_size], parts.at[k], across[k - 1])
    square_parts[0] = squares[...]
    total = terms[col].astype(jnp.float32)
    for k in range(1, mdl_size):
        copies.arrive(("s", k), square_parts.at[k], across[0])
    stacked = square_parts[...].reshape(mdl_size * 8, tokens)
    ones = jnp.full((mdl_size * 8, columns), 0.125, jnp.float32)
    mean = lax.dot_general(
        stacked,
        ones,
        (((0,), (0,)), ((), ())),
        preferred_element_type=jnp.float32,
        precision=HIGH,
    ) / (mdl_size * 512)
    scale = lax.rsqrt(mean + EPSILON)
    for k in sorted(range(1, mdl_size), key=lambda k: min(k, mdl_size - k)):
        copies.arrive(("t", k), parts.at[k], across[0])
        total = total + parts[k].astype(jnp.float32)
    result[...] = (total * scale).astype(jnp.bfloat16).reshape(per_dev, draft, columns)
    for s in range(SLOTS):
        outgoing[s] = result[page_of[s]]
    for o in range(1, WINDOW):
        part = pl.ds(o * CAP, CAP)
        copies.send(("r", o), outgoing.at[part], incoming.at[part], behind[o - 1])
    incoming[0:CAP] = outgoing[0:CAP]
    for o in range(1, WINDOW):
        copies.arrive(("r", o), incoming.at[pl.ds(o * CAP, CAP)], across[0])
    for q in range(per_dev):
        mixed[q] = incoming[slot_of[q]]
    copies.finish()


def give_back(page_of, slot_of, terms, squares, per_dev, groups, mdl_size):
    _, tokens, columns = terms.shape
    draft = tokens // per_dev
    bf16 = jnp.bfloat16
    count = 2 * mdl_size + WINDOW
    vmem = pl.BlockSpec(memory_space=pltpu.VMEM)
    smem = pl.BlockSpec(memory_space=pltpu.SMEM)
    return pl.pallas_call(
        functools.partial(return_kernel, groups, mdl_size),
        out_shape=jax.ShapeDtypeStruct((per_dev, draft, columns), bf16),
        in_specs=[smem, smem, vmem, vmem],
        out_specs=vmem,
        scratch_shapes=[
            pltpu.VMEM((mdl_size, tokens, columns), bf16),
            pltpu.VMEM((mdl_size, 8, tokens), jnp.float32),
            pltpu.VMEM((per_dev, draft, columns), bf16),
            pltpu.VMEM((SLOTS, draft, columns), bf16),
            pltpu.VMEM((SLOTS, draft, columns), bf16),
            pltpu.SemaphoreType.DMA((count,)),
            pltpu.SemaphoreType.DMA((count,)),
        ],
        compiler_params=pltpu.CompilerParams(collective_id=1, has_side_effects=True),
        name="sum_and_return_rows",
    )(page_of, slot_of, terms, squares)


def on_device(
    hidden_in,
    z_weight,
    x_weight,
    state_proj,
    step_weight,
    step_bias,
    decay_log,
    skip_gain,
    conv_inner,
    conv_state,
    norm_gain,
    out_weight,
    state_pool,
    conv_pool_inner,
    conv_pool_state,
    owner_dev,
    state_page,
    conv_page,
    accepted,
):
    groups = lax.axis_size("req")
    mdl_size = lax.axis_size("mdl")
    this_dev = lax.axis_index("req")
    per_dev, heads = state_pool.shape[0], state_pool.shape[1]
    tokens, depth = hidden_in.shape
    draft = tokens // per_dev
    slot_of, source_of, pick_from, page_of, conv_of, kept = route_tables(
        owner_dev, state_page, conv_page, accepted, groups, per_dev, this_dev
    )
    shard = jnp.concatenate(
        [
            z_weight,
            x_weight,
            state_proj,
            jnp.pad(step_weight, ((0, 0), (0, 128 - heads))),
            out_weight.T,
        ],
        axis=1,
    )
    rows_shard, packed = shard.shape
    full, rows_full = gather(
        source_of,
        pick_from,
        hidden_in.reshape(per_dev, draft, depth),
        shard.reshape(2, rows_shard // 2, packed),
        groups,
        mdl_size,
    )
    terms, squares, new_states, edge_inner, edge_state = mix(
        conv_of,
        kept,
        step_bias,
        decay_log,
        skip_gain,
        rows_full,
        full.reshape(groups * rows_shard, packed),
        conv_inner,
        conv_state,
        norm_gain.reshape(1, -1),
        state_pool,
        conv_pool_inner.transpose(1, 0, 2),
        conv_pool_state.transpose(1, 0, 2),
    )
    mixed = give_back(page_of, slot_of, terms, squares, per_dev, groups, mdl_size)
    return (
        mixed.reshape(tokens, -1),
        new_states,
        edge_inner.transpose(1, 0, 2),
        edge_state.transpose(1, 0, 2),
    )


def solution(mesh):
    return jax.shard_map(
        on_device,
        mesh=mesh,
        in_specs=(
            P("req", None),
            P("req", "mdl"),
            P("req", "mdl"),
            P("req", None),
            P("req", "mdl"),
            P("mdl"),
            P("mdl"),
            P("mdl"),
            P(None, "mdl"),
            P(),
            P("mdl"),
            P("mdl", "req"),
            P("req", "mdl", None, None),
            P("req", None, "mdl"),
            P("req", None, None),
            P(),
            P(),
            P(),
            P(),
        ),
        out_specs=(
            P("req", "mdl"),
            P("req", "mdl", None, None),
            P("req", None, "mdl"),
            P("req", None, None),
        ),
        check_vma=False,
    )
```

time: 402 us -> 116 us (0.29)
  waiting for transfers between devices: 206 us -> 0 us
  Pallas kernels: 0 us -> 90.6 us
  blocking collectives: 70.7 us -> 0 us
  starting transfers between devices: 47.6 us -> 0 us
  matrix products: 27.8 us -> 0 us
  between operations: 14.7 us -> 0.72 us
  other arithmetic: 10.6 us -> 3.53 us
    all_gather x4 -> x0, waiting for transfers between devices: 178 us -> none  [the longest x1 82.4 us: project_in(): lax.all_gather(x_weight, 'req', axis=0, tiled=True)]
    pallas_call x0 -> x3, Pallas kernels: none -> 90.6 us  [the longest x1 58.9 us: gather(): pl.pallas_call(functools.partial(gather_kernel, groups, mdl_size), out_sh...]
    all_gather x1 -> x0, blocking collectives: 57 us -> none  [project_in(): lax.all_gather(step_weight, 'req', axis=0, tiled=True)]
    ppermute x16 -> x0, starting transfers between devices: 47.4 us -> none  [from_behind(): return lax.ppermute(value, axis, pairs)]
    dot_general x15 -> x0, matrix products: 27.8 us -> none  [the longest x4 6.56 us: project_in(): jnp.dot(rows, piece, preferred_element_type=jnp.float32)]
    reduce_scatter x1 -> x0, waiting for transfers between devices: 20.3 us -> none  [finish(): lax.psum_scatter(terms, 'mdl', scatter_dimension=1, tiled=True)]
    unnamed x71 -> x38, local copies, waits for them, and re-layouts: 1.41 us -> 17.8 us
    psum x1 -> x0, blocking collectives: 13.7 us -> none  [finish(): squares = lax.psum(jnp.sum(gated * gated, axis=1), 'mdl')]
  transfers between devices with their start and end apart: 21 -> 0, of which waited for: 8 -> 0; matrix products, arithmetic and copies ran while one was open for 13% -> 0% of each run, Pallas kernels for 0% -> 0%
where the time goes in v1:
time: 116 us; the launch traced here: 115 us
  Pallas kernels  90.6 us (78%)
  local copies, waits for them, and re-layouts  19.9 us (17%)
  other arithmetic  3.53 us (3%)
    pallas_call x1, Pallas kernels, gather(): pl.pallas_call(functools.partial(gather_kernel, groups, mdl_size), out_sh...  58.9 us
    pallas_call x1, Pallas kernels, give_back(): pl.pallas_call(functools.partial(return_kernel, groups, mdl_size), out_sh...  24.4 us
    unnamed x38, local copies, waits for them, and re-layouts  17.8 us
    pallas_call x1, Pallas kernels, mix(): pl.pallas_call(functools.partial(mix_kernel, (per_dev, draft, heads, hdim...  7.32 us

profile of v1, /device:TPU:1, one launch (start us, length us, event | category | flops | bytes accessed | tf_op | source)
XLA Modules:
  0.0 114.7 jit_solution(7000836410644072559)
XLA Ops:
  0.6 0.7 broadcast_compare_fusion
  1.3 0.8 copy.34
  2.1 0.8 eq.69
  2.9 0.1 convert_reduce_fusion
  3.0 0.2 dynamic-slice_reduce_fusion.slot_of
  3.2 0.6 select_reduce_fusion.3.source_of
  3.9 0.1 reduce_sum.57
  4.1 0.7 fusion.6
  4.8 0.9 select_reduce_fusion
  5.7 0.6 select_reduce_fusion.4.page_of
  6.3 0.8 constant_dynamic-update-slice_fusion.3
  7.0 0.8 constant_dynamic-update-slice_fusion.2
  7.8 0.7 constant_dynamic-update-slice_fusion.1
  8.5 0.8 bitcast_dynamic-update-slice_fusion
  9.3 0.6 copy-done.13
  9.9 58.9 %gather_rows_and_weights.1 = (bf16[8,4,2,2,16,1920]{5,4,3,2,1,0:T(8,128)(2,1)}, bf16[8,8,16,256]{3,2,1,0:T(8,128)(2,1)}) custom-call(s32[16]{0:T(128)} %select_reduce_fusion.3.source_of, s32[8]{0:T(128)} %copy-done.15, bf16[8,16,2048]{2,1,0:T(8,128)(2,1)} %bitcast.15, bf16[2,16,1920]{2,1,0:T(8,128)(2,1)} %bitcast.17), custom_call_target="tpu_custom_call" | custom-call | tf_op jit(solution)/shard_map/gather_rows_and_weights/pallas_call | solution.py:243
  68.8 3.2 %copy-done = bf16[8,4,2,2,16,1920]{5,4,3,2,1,0:T(8,128)(2,1)S(1)} copy-done((bf16[8,4,2,2,16,1920]{5,4,3,2,1,0:T(8,128)(2,1)S(1)}, bf16[8,4,2,2,16,1920]{5,4,3,2,1,0:T(8,128)(2,1)}, u32[]{:S(2)}) %copy-start) | copy-done | bytes 7864344
  72.0 1.6 %copy-done.1 = f32[8,8,64,128]{3,2,1,0:T(8,128)S(1)} copy-done((f32[8,8,64,128]{3,2,1,0:T(8,128)S(1)}, f32[8,8,64,128]{3,2,1,0:T(8,128)}, u32[]{:S(2)}) %copy-start.1) | copy-done | bytes 2097176
  73.6 1.0 copy-done.2
  74.7 0.7 copy-done.4
  75.4 0.7 copy-done.5
  76.1 0.7 copy-done.6
  76.8 0.7 copy-done.7
  77.5 0.7 copy-done.9
  78.2 0.7 copy-done.10
  78.8 0.7 copy-done.11
  79.5 0.7 copy-done.12
  80.1 7.3 %project_and_mix.1 = (bf16[8,128,256]{2,1,0:T(8,128)(2,1)S(1)}, f32[8,128]{1,0:T(8,128)S(1)}, f32[8,8,64,128]{3,2,1,0:T(8,128)}, bf16[3,8,512]{2,1,0:T(8,128)(2,1)}, bf16[3,8,256]{2,1,0:T(8,128)(2,1)}) custom-call(s32[8]{0:T(128)S(1)} %get-tuple-element.19.conv_of, s32[8]{0:T(128)S(1)} %get-tuple-element.18.kept, f32[8]{0:T(128)S(1)} %copy-done.10, ...), custom_call_target="tpu_custom_call" | custom-call | tf_op jit(solution)/shard_map/project_and_mix/pallas_call | solution.py:471
  87.5 0.8 copy-done.3
  88.3 0.6 copy-done.8
  88.8 24.4 %sum_and_return_rows.1 = bf16[8,16,256]{2,1,0:T(8,128)(2,1)} custom-call(s32[16]{0:T(128)} %select_reduce_fusion.4.page_of, s32[8]{0:T(128)} %copy-done.14, bf16[8,128,256]{2,1,0:T(8,128)(2,1)} %copy-done.3, f32[8,128]{1,0:T(8,128)} %copy-done.8), custom_call_target="tpu_custom_call" | custom-call | tf_op jit(solution)/shard_map/sum_and_return_rows/pallas_call | solution.py:582
  113.2 1.5 %copy.40 = bf16[128,256]{1,0:T(8,128)(2,1)} copy(bf16[128,256]{1,0:T(8,128)(2,1)} %bitcast.16) | data formatting | bytes 131072
  (25 shorter events, 0.3 us)
Async XLA Ops:
  3.2 84.2 %copy-start.14 = (s32[8]{0:T(128)}, s32[8]{0:T(128)S(1)}, u32[]{:S(2)}) copy-start(s32[8]{0:T(128)S(1)} %dynamic-slice_reduce_fusion.slot_of) | copy-start | bytes 100
  5.7 3.6 %copy-start.15 = (s32[8]{0:T(128)}, s32[8]{0:T(128)S(1)}, u32[]{:S(2)}) copy-start(s32[8]{0:T(128)S(1)} %get-tuple-element.20.pick_from) | copy-start | bytes 100
  9.3 0.6 copy-start.13
  68.8 3.2 %copy-start = (bf16[8,4,2,2,16,1920]{5,4,3,2,1,0:T(8,128)(2,1)S(1)}, bf16[8,4,2,2,16,1920]{5,4,3,2,1,0:T(8,128)(2,1)}, u32[]{:S(2)}) copy-start(bf16[8,4,2,2,16,1920]{5,4,3,2,1,0:T(8,128)(2,1)} %get-tuple-element.12) | copy-start | bytes 23592964
  72.0 1.6 %copy-start.1 = (f32[8,8,64,128]{3,2,1,0:T(8,128)S(1)}, f32[8,8,64,128]{3,2,1,0:T(8,128)}, u32[]{:S(2)}) copy-start(f32[8,8,64,128]{3,2,1,0:T(8,128)} %state_pool.1) | copy-start | bytes 6291460
  73.6 1.0 copy-start.2
  74.7 0.7 copy-start.4
  75.4 0.7 copy-start.5
  76.1 0.7 copy-start.6
  76.8 0.7 copy-start.7
  77.5 0.7 copy-start.9
  78.2 0.7 copy-start.10
  78.8 0.7 copy-start.11
  79.5 0.7 copy-start.12
  87.5 0.8 copy-start.3
  88.3 0.6 copy-start.8

commit v2 on v0

v2 whole, which is shorter than its diff:
```python
import functools

import jax
import jax.numpy as jnp
from jax import lax
from jax.experimental import pallas as pl
from jax.experimental.pallas import tpu as pltpu
from jax.sharding import PartitionSpec as P

KCONV = 4
CAP = 2
WINDOW = 8
SLOTS = WINDOW * CAP
XN = 4
PAD = 128
HIGH = lax.Precision.HIGHEST
EPSILON = 1e-05
MESH = pl.DeviceIdType.MESH
NT = (((1,), (1,)), ((), ()))
TN = (((0,), (0,)), ((), ()))


def dot(a, b, precision=None):
    return jnp.dot(a, b, preferred_element_type=jnp.float32, precision=precision)


def dot_nt(a, b, precision=None):
    return lax.dot_general(a, b, NT, preferred_element_type=jnp.float32, precision=precision)


class Copies:
    def __init__(self, send_sem, recv_sem, anyone):
        self.send_sem, self.recv_sem, self.anyone = send_sem, recv_sem, anyone
        self.keys, self.groups = {}, {}

    def describe(self, name, group, src, dst, peer):
        k = self.keys.setdefault(name, len(self.keys))
        g = self.groups.setdefault(group, len(self.groups))
        return pltpu.make_async_remote_copy(
            src_ref=src,
            dst_ref=dst,
            send_sem=self.send_sem.at[g],
            recv_sem=self.recv_sem.at[k],
            device_id=peer,
            device_id_type=MESH,
        )

    def send(self, name, group, src, dst, peer):
        self.describe(name, group, src, dst, peer).start()

    def arrive(self, name, group, where):
        self.describe(name, group, where, where, self.anyone).wait_recv()

    def sent(self, group, whole):
        pltpu.make_async_copy(whole, whole, self.send_sem.at[self.groups[group]]).wait()


def layer_kernel(
    groups,
    mdl_size,
    owner_dev,
    state_page,
    conv_page,
    accepted,
    step_bias,
    decay_log,
    skip_gain,
    z_weight,
    x_weight,
    state_proj,
    step_t,
    out_t,
    conv_inner,
    conv_state,
    norm_gain,
    hist_inner,
    hist_state,
    hidden,
    state_pool,
    mixed,
    new_states,
    edge_inner,
    edge_state,
    full_a,
    full_b,
    rows_full,
    slice_in,
    outgoing,
    incoming,
    state,
    acc_a,
    acc_b,
    series_x,
    series_s,
    hist_x,
    hist_s,
    edge_x,
    edge_s,
    carried,
    table,
    decay_s,
    terms,
    squares,
    parts,
    square_parts,
    result,
    outgoing2,
    incoming2,
    send_sem,
    recv_sem,
    local_sem,
):
    f32, bf16 = jnp.float32, jnp.bfloat16
    per_dev, draft, columns = mixed.shape
    tokens = per_dev * draft
    heads, hdim, nstate = state.shape[1:]
    inner = heads * hdim
    width = slice_in.shape[2]
    zn = groups // (2 * XN)
    me = lax.axis_index("req")
    col = lax.axis_index("mdl")
    core = me % 2
    x = (me // 2) % XN
    z = me // (2 * XN)

    def zi(v):
        return (v + zn) % zn

    def xi(v):
        return (v + XN) % XN

    def at(zz, xx):
        return {"req": (zi(zz) * XN + xi(xx)) * 2 + core}

    load_rows = pltpu.make_async_copy(
        hidden.at[:, :, pl.ds(pl.multiple_of(col * width, width), width)],
        slice_in,
        local_sem.at[0],
    )
    load_rows.start()
    load_state = pltpu.make_async_copy(state_pool, state, local_sem.at[1])
    load_state.start()

    sibling = {"req": me + 1 - 2 * core}
    up, down = at(z + 1, x), at(z - 1, x)
    right, left_x = at(z, x + 1), at(z, x - 1)
    xs = [at(z, x + d) for d in range(1, XN)]
    ahead = [{"req": (me + o) % groups} for o in range(1, WINDOW)]
    behind = [{"req": (me - o + groups) % groups} for o in range(1, WINDOW)]
    across = [{"mdl": (col + k) % mdl_size} for k in range(1, mdl_size)]
    peers = [sibling, up, down] + xs + ahead + behind + across
    barrier = pltpu.get_barrier_semaphore()
    for peer in peers:
        pl.semaphore_signal(barrier, inc=1, device_id=peer, device_id_type=MESH)

    full_a[z, x, core, :, :inner] = z_weight[...]
    full_a[z, x, core, :, inner:] = state_proj[...]
    full_b[z, x, core, :, :inner] = x_weight[...]
    place = (
        lax.broadcasted_iota(jnp.int32, (heads, PAD), 0)
        == lax.broadcasted_iota(jnp.int32, (heads, PAD), 1)
    ).astype(f32)
    full_b[z, x, core, :, inner : inner + PAD] = lax.dot_general(
        step_t[...].astype(f32), place, TN, preferred_element_type=f32, precision=HIGH
    ).astype(bf16)
    full_b[z, x, core, :, inner + PAD :] = out_t[...]
    pl.semaphore_wait(barrier, len(peers))

    copies = Copies(send_sem, recv_sem, up)
    half = zn // 2
    rows = full_a.shape[3]
    halves = (pl.ds(0, rows // 2), pl.ds(rows // 2, rows // 2))
    order = [0]
    for s in range(1, half):
        order += [-s, s]
    order.append(-half)
    place_of = {d: n for n, d in enumerate(order)}

    def piece_a(dz, dx):
        return full_a.at[zi(z + dz), xi(x + dx), core]

    def piece_b(dz, dx):
        return full_b.at[zi(z + dz), xi(x + dx), core]

    def a_up(s, d):
        group = "a_last" if s == half else "a"
        copies.send(("au", s, d), group, piece_a(1 - s, -d), piece_a(1 - s, -d), up)

    def a_down(s, d):
        group = "a_last" if s == half else "a"
        copies.send(("ad", s, d), group, piece_a(s - 1, -d), piece_a(s - 1, -d), down)

    up_last, down_last = range(0, XN // 2), range(XN // 2, XN)

    def b_up(s):
        p = piece_b(1 - s, 0)
        if s == half:
            copies.send(("bu", s), "b_last", p.at[halves[0]], p.at[halves[0]], up)
        else:
            copies.send(("bu", s), "b", p, p, up)

    def b_down(s):
        p = piece_b(s - 1, 0)
        if s == half:
            copies.send(("bd", s), "b_last", p.at[halves[1]], p.at[halves[1]], down)
        else:
            copies.send(("bd", s), "b", p, p, down)

    def b_side(n):
        p = piece_b(order[n], 0)
        copies.send(("br", n), "bx", p, p, right)
        copies.send(("bl", n), "bx", p, p, left_x)

    def e_ax(d):
        copies.arrive(("ax", d), "ax", piece_a(0, -d))
        a_up(1, d)
        a_down(1, d)

    def e_bz(s):
        if s < half:
            copies.arrive(("bu", s), "b", piece_b(-s, 0))
            b_up(s + 1)
            b_side(place_of[-s])
            copies.arrive(("bd", s), "b", piece_b(s, 0))
            b_down(s + 1)
            b_side(place_of[s])
        else:
            copies.arrive(("bu", s), "b_last", piece_b(-s, 0).at[halves[0]])
            copies.arrive(("bd", s), "b_last", piece_b(-s, 0).at[halves[1]])
            b_side(place_of[-s])

    def e_a(s, d):
        if s < half:
            copies.arrive(("au", s, d), "a", piece_a(-s, -d))
            if s + 1 < half or d in up_last:
                a_up(s + 1, d)
            copies.arrive(("ad", s, d), "a", piece_a(s, -d))
            if s + 1 < half or d in down_last:
                a_down(s + 1, d)
        elif d in up_last:
            copies.arrive(("au", s, d), "a_last", piece_a(-s, -d))
        else:
            copies.arrive(("ad", s, d), "a_last", piece_a(-s, -d))

    def e_bx(n):
        copies.arrive(("br", n), "bx", piece_b(order[n], -1))
        copies.arrive(("bl", n), "bx", piece_b(order[n], 1))
        if n % 2 == 0:
            p = piece_b(order[n], -1)
            copies.send(("bf", n), "bf", p, p, right)
        else:
            p = piece_b(order[n], 1)
            copies.send(("bf", n), "bf", p, p, left_x)

    def e_bf(n):
        copies.arrive(("bf", n), "bf", piece_b(order[n], 2))

    def e_sib(n):
        a = full_a.at[zi(z + order[n]), :, core]
        b = full_b.at[zi(z + order[n]), :, core]
        copies.send(("sa", n), "sa", a, a, sibling)
        copies.send(("sb", n), "sb", b, b, sibling)

    def e_proj(n):
        zz = zi(z + order[n])
        copies.arrive(("sa", n), "sa", full_a.at[zz, :, 1 - core])
        copies.arrive(("sb", n), "sb", full_b.at[zz, :, 1 - core])
        blk = rows_full[zz].reshape(tokens, width)
        part_a = dot(blk, full_a[zz].reshape(width, full_a.shape[4]))
        part_b = dot(blk, full_b[zz, :, :, :, : inner + PAD].reshape(width, inner + PAD))
        if n == 0:
            acc_a[...] = part_a
            acc_b[...] = part_b
        else:
            acc_a[...] += part_a
            acc_b[...] += part_b

    def e_rows():
        for o in range(1, WINDOW):
            copies.arrive(("h", o), "h", incoming.at[pl.ds(o * CAP, CAP)])
        by_page = [jnp.int32(0)] * per_dev
        by_conv = [jnp.int32(0)] * per_dev
        for o in range(WINDOW):
            base = ((me - o + groups) % groups) * per_dev
            seen = jnp.int32(0)
            pages = [jnp.int32(0)] * CAP
            for q in range(per_dev):
                hit = owner_dev[base + q] == me
                page = jnp.where(hit, state_page[base + q], -1)
                conv = jnp.where(hit, conv_page[base + q], -1)
                kept = accepted[base + q]
                info = (o * CAP + seen) + conv * 64 + kept * 1024
                back = page + kept * 1024
                for p in range(per_dev):
                    by_page[p] = jnp.where(page == p, info, by_page[p])
                    by_conv[p] = jnp.where(conv == p, back, by_conv[p])
                for c in range(CAP):
                    pages[c] = jnp.where(hit & (seen == c), page, pages[c])
                seen = seen + hit.astype(jnp.int32)
            for c in range(CAP):
                table[8 + o * CAP + c] = pages[c]
        for p in range(per_dev):
            table[24 + p] = jnp.minimum(by_page[p] & 63, SLOTS - 1)
            table[32 + p] = jnp.minimum((by_page[p] >> 6) & 15, per_dev - 1)
            table[40 + p] = jnp.minimum(by_page[p] >> 10, draft)
            table[48 + p] = jnp.minimum(by_conv[p] & 1023, per_dev - 1)
            table[56 + p] = jnp.minimum(by_conv[p] >> 10, draft)
        for p in range(per_dev):
            rows_full[col, p] = incoming[table[24 + p]]
        for k in range(1, mdl_size):
            copies.send(("y", k), "y", rows_full.at[col], rows_full.at[col], across[k - 1])

    def e_rows_in():
        for k in range(1, mdl_size):
            copies.arrive(("y", k), "y", rows_full.at[(col - k + mdl_size) % mdl_size])

    own_a, own_b = piece_a(0, 0), piece_b(0, 0)
    b_up(1)
    b_down(1)
    for d in range(1, XN):
        copies.send(("ax", d), "ax", own_a, own_a, xs[d - 1])
    b_side(0)
    a_up(1, 0)
    a_down(1, 0)

    owners = [owner_dev[me * per_dev + q] for q in range(per_dev)]
    slots = []
    for q in range(per_dev):
        offset = owners[q] - me
        offset = jnp.where(offset < 0, offset + groups, offset)
        rank = jnp.int32(0)
        for r in range(q):
            rank = rank + (owners[r] == owners[q]).astype(jnp.int32)
        slots.append(offset * CAP + rank)
        table[q] = jnp.minimum(slots[q], SLOTS - 1)
    load_rows.wait()
    for s in range(SLOTS):
        source = jnp.int32(0)
        for q in range(per_dev):
            source = jnp.where(slots[q] == s, q, source)
        outgoing[s] = slice_in[source]
    for o in range(1, WINDOW):
        part = pl.ds(o * CAP, CAP)
        copies.send(("h", o), "h", outgoing.at[part], incoming.at[part], ahead[o - 1])
    incoming[0:CAP] = outgoing[0:CAP]

    events = []
    for d, t in ((1, 2.0), (3, 2.1), (2, 3.0)):
        events.append((t, "ax", functools.partial(e_ax, d)))
    for s in range(1, half + 1):
        events.append((0.4 + 2.2 * s, "bz", functools.partial(e_bz, s)))
        for j, d in enumerate((0, 1, 3, 2)):
            events.append((2.6 + 5.0 * (s - 1) + 1.2 * j, "a", functools.partial(e_a, s, d)))
    for n in range(zn):
        t_bx = 3.4 + 2.2 * n
        t_a = 4.0 if n == 0 else 6.3 + 5.0 * (abs(order[n]) - 1)
        t_sib = max(t_bx + 2.5, t_a + 0.01)
        events.append((t_bx, "bx", functools.partial(e_bx, n)))
        events.append((t_bx + 2.5, "bf", functools.partial(e_bf, n)))
        events.append((t_sib + 0.02, "sib", functools.partial(e_sib, n)))
        events.append((max(t_sib + 2.0, 16.0), "proj", functools.partial(e_proj, n)))
    events.append((4.5, "rows", e_rows))
    events.append((15.9, "in", e_rows_in))
    events.sort(key=lambda e: e[0])
    for _, _, run in events:
        run()

    hist_x[...] = hist_inner[...].astype(f32)
    hist_s[...] = hist_state[...].astype(f32)
    lead = 8 - (KCONV - 1)
    series_x[:, 8:, :] = acc_b[:, :inner].astype(bf16).astype(f32).reshape(per_dev, draft, inner)
    series_s[:, 8:, :] = (
        acc_a[:, inner:].astype(bf16).astype(f32).reshape(per_dev, draft, 2 * nstate)
    )
    for p in range(per_dev):
        for j in range(KCONV - 1):
            series_x[p, lead + j : lead + j + 1, :] = hist_x[j, pl.ds(table[32 + p], 1), :]
            series_s[p, lead + j : lead + j + 1, :] = hist_s[j, pl.ds(table[32 + p], 1), :]

    def conv(series, taps):
        total = taps[0:1, :] * series[:, lead : lead + draft, :]
        for k in range(1, KCONV):
            total = total + taps[k : k + 1, :] * series[:, lead + k : lead + k + draft, :]
        return jax.nn.silu(total).reshape(tokens, total.shape[2])

    active = conv(series_x, conv_inner)
    maps = conv(series_s, conv_state)
    b_rows, c_rows = maps[:, :nstate], maps[:, nstate:]

    lane = lax.broadcasted_iota(jnp.int32, (1, PAD), 1)
    bias_row = jnp.zeros((1, PAD), f32)
    rate_row = jnp.zeros((1, PAD), f32)
    for h in range(heads):
        bias_row = jnp.where(lane == h, step_bias[h], bias_row)
        rate_row = jnp.where(lane == h, decay_log[h], rate_row)
    rate_row = jnp.exp(rate_row)
    step_raw = acc_b[:, inner:].astype(bf16).astype(f32)
    size = jax.nn.softplus(step_raw + bias_row)
    rows_i = lax.broadcasted_iota(jnp.int32, (tokens, tokens), 0)
    cols_i = lax.broadcasted_iota(jnp.int32, (tokens, tokens), 1)
    causal = (rows_i // draft == cols_i // draft) & (cols_i <= rows_i)
    decay = dot(causal.astype(f32), -size * rate_row, HIGH)
    decay_t, size_t = decay.T, size.T
    scores = dot_nt(c_rows, b_rows, HIGH)
    end_at = jnp.zeros((tokens, tokens), jnp.int32)
    for p in range(per_dev):
        end_at = jnp.where(rows_i // draft == p, p * draft + table[40 + p] - 1, end_at)
    end_decay = dot((cols_i == end_at).astype(f32), decay, HIGH)
    before = rows_i <= end_at
    chosen_w = jnp.where(before, jnp.exp(jnp.where(before, end_decay - decay, 0.0)), 0.0) * size
    grown = jnp.exp(decay)
    decay_s[...] = jnp.exp(end_decay)

    b_low = b_rows.astype(bf16)
    c_low = c_rows.astype(bf16)
    load_state.wait()
    for p in range(per_dev):
        start = state[p].reshape(inner, nstate)
        carried[p * draft : (p + 1) * draft, :] = dot_nt(
            c_low[p * draft : (p + 1) * draft, :], start.astype(bf16)
        )

    left = lax.broadcasted_iota(jnp.int32, (tokens, PAD), 1) < hdim

    def spread(values, j):
        return jnp.where(left, values[:, 2 * j : 2 * j + 1], values[:, 2 * j + 1 : 2 * j + 2])

    total = jnp.zeros((tokens, PAD), f32)
    gated_cols = []
    for j in range(heads // 2):
        cols = slice(j * PAD, (j + 1) * PAD)
        x_pair = active[:, cols]
        x_low = x_pair.astype(bf16)
        pair = []
        for h in (2 * j, 2 * j + 1):
            gap = decay[:, h : h + 1] - decay_t[h : h + 1, :]
            weight = jnp.exp(jnp.where(causal, gap, -1e30)) * scores * size_t[h : h + 1, :]
            pair.append(dot(weight.astype(bf16), x_low))
        skip = jnp.where(left, skip_gain[2 * j], skip_gain[2 * j + 1])
        y = (
            jnp.where(left, pair[0], pair[1])
            + carried[:, cols] * spread(grown, j)
            + skip * x_pair
        )
        gated = y.astype(bf16).astype(f32) * jax.nn.silu(acc_a[:, cols])
        total = total + gated * gated
        gated_cols.append((gated * norm_gain[0:1, cols]).astype(bf16))
    gated_low = jnp.concatenate(gated_cols, axis=1)
    squares[...] = dot_nt(jnp.ones((8, PAD), f32), total, HIGH)
    for k in range(1, mdl_size):
        copies.send(("s", k), "s", squares, square_parts.at[k], across[k - 1])
    far_first = sorted(range(1, mdl_size), key=lambda k: -min(k, mdl_size - k))

    def project_out(m):
        block = full_b[m, :, :, :, inner + PAD :].reshape(columns, inner)
        return dot_nt(gated_low, block)

    for k in far_first:
        m = (col + k) % mdl_size
        terms[k] = project_out(m).astype(bf16)
        copies.send(("t", k), "t", terms.at[k], parts.at[k], across[k - 1])
    own_term = project_out(col)

    picked_t = []
    for j in range(heads // 2):
        cols = slice(j * PAD, (j + 1) * PAD)
        picked_t.append((active[:, cols] * spread(chosen_w, j)).T.astype(bf16))
    picked = jnp.concatenate(picked_t, axis=0)
    row_of = lax.broadcasted_iota(jnp.int32, (tokens, nstate), 0) // draft
    stores = []
    for p in range(per_dev):
        added = dot(picked, jnp.where(row_of == p, b_low, jnp.zeros_like(b_low)))
        for h in range(heads):
            factor = decay_s[p * draft : p * draft + 1, h : h + 1]
            state[p, h] = factor * state[p, h] + added[h * hdim : (h + 1) * hdim, :]
        store = pltpu.make_async_copy(state.at[p], new_states.at[p], local_sem.at[2 + p])
        store.start()
        stores.append(store)
    for c in range(per_dev):
        for j in range(KCONV - 1):
            row = pl.ds(lead + table[56 + c] + j, 1)
            edge_x[j, c : c + 1, :] = series_x[table[48 + c], row, :]
            edge_s[j, c : c + 1, :] = series_s[table[48 + c], row, :]
    edge_inner[...] = edge_x[...].astype(bf16)
    edge_state[...] = edge_s[...].astype(bf16)

    square_parts[0] = squares[...]
    for k in range(1, mdl_size):
        copies.arrive(("s", k), "s", square_parts.at[k])
    stacked = square_parts[...].reshape(mdl_size * 8, tokens)
    eighth = jnp.full((mdl_size * 8, columns), 0.125, f32)
    mean = lax.dot_general(
        stacked, eighth, TN, preferred_element_type=f32, precision=HIGH
    ) / (mdl_size * inner)
    scale = lax.rsqrt(mean + EPSILON)
    for k in reversed(far_first):
        copies.arrive(("t", k), "t", parts.at[k])
        own_term = own_term + parts[k].astype(f32)
    result[...] = (own_term * scale).astype(bf16).reshape(per_dev, draft, columns)
    for s in range(SLOTS):
        outgoing2[s] = result[table[8 + s]]
    for o in range(1, WINDOW):
        part = pl.ds(o * CAP, CAP)
        copies.send(("r", o), "r", outgoing2.at[part], incoming2.at[part], behind[o - 1])
    incoming2[0:CAP] = outgoing2[0:CAP]

    copies.sent("a", full_a.at[pl.ds(0, half - 1)])
    copies.sent("a_last", full_a.at[0, pl.ds(0, 2)])
    copies.sent("ax", full_a.at[0, pl.ds(0, XN - 1), 0])
    copies.sent("b", full_b.at[0, pl.ds(0, half - 1)])
    copies.sent("b_last", full_b.at[0, 0, 0])
    copies.sent("bx", full_b.at[pl.ds(0, 2)])
    copies.sent("bf", full_b.at[0])
    copies.sent("sa", full_a.at[pl.ds(0, half)])
    copies.sent("sb", full_b.at[pl.ds(0, half)])
    copies.sent("h", incoming.at[pl.ds(CAP, SLOTS - CAP)])
    copies.sent("y", rows_full.at[pl.ds(1, mdl_size - 1)])
    copies.sent("s", square_parts.at[pl.ds(1, mdl_size - 1)])
    copies.sent("t", parts.at[pl.ds(1, mdl_size - 1)])
    for store in stores:
        store.wait()
    for o in range(1, WINDOW):
        copies.arrive(("r", o), "r", incoming2.at[pl.ds(o * CAP, CAP)])
    for q in range(per_dev):
        mixed[q] = incoming2[table[q]]
    copies.sent("r", incoming2.at[pl.ds(CAP, SLOTS - CAP)])


def on_device(
    hidden_in,
    z_weight,
    x_weight,
    state_proj,
    step_weight,
    step_bias,
    decay_log,
    skip_gain,
    conv_inner,
    conv_state,
    norm_gain,
    out_weight,
    state_pool,
    conv_pool_inner,
    conv_pool_state,
    owner_dev,
    state_page,
    conv_page,
    accepted,
):
    groups = lax.axis_size("req")
    mdl_size = lax.axis_size("mdl")
    per_dev, heads, hdim, nstate = state_pool.shape
    tokens, depth = hidden_in.shape
    draft = tokens // per_dev
    inner = heads * hdim
    zn = groups // (2 * XN)
    rows = z_weight.shape[0]
    width = depth // mdl_size
    columns = depth // mdl_size
    f32, bf16 = jnp.float32, jnp.bfloat16
    smem = pl.BlockSpec(memory_space=pltpu.SMEM)
    vmem = pl.BlockSpec(memory_space=pltpu.VMEM)
    hbm = pl.BlockSpec(memory_space=pl.ANY)
    hist_inner = conv_pool_inner.transpose(1, 0, 2)
    hist_state = conv_pool_state.transpose(1, 0, 2)
    edge = (KCONV - 1, per_dev)
    mixed, new_states, edge_inner, edge_state = pl.pallas_call(
        functools.partial(layer_kernel, groups, mdl_size),
        out_shape=(
            jax.ShapeDtypeStruct((per_dev, draft, columns), bf16),
            jax.ShapeDtypeStruct(state_pool.shape, state_pool.dtype),
            jax.ShapeDtypeStruct(hist_inner.shape, hist_inner.dtype),
            jax.ShapeDtypeStruct(hist_state.shape, hist_state.dtype),
        ),
        in_specs=[smem] * 7 + [vmem] * 10 + [hbm] * 2,
        out_specs=(vmem, hbm, vmem, vmem),
        scratch_shapes=[
            pltpu.VMEM((zn, XN, 2, rows, inner + 2 * nstate), bf16),
            pltpu.VMEM((zn, XN, 2, rows, 2 * inner + PAD), bf16),
            pltpu.VMEM((mdl_size, per_dev, draft, width), bf16),
            pltpu.VMEM((per_dev, draft, width), bf16),
            pltpu.VMEM((SLOTS, draft, width), bf16),
            pltpu.VMEM((SLOTS, draft, width), bf16),
            pltpu.VMEM(state_pool.shape, f32),
            pltpu.VMEM((tokens, inner + 2 * nstate), f32),
            pltpu.VMEM((tokens, inner + PAD), f32),
            pltpu.VMEM((per_dev, draft + 8, inner), f32),
            pltpu.VMEM((per_dev, draft + 8, 2 * nstate), f32),
            pltpu.VMEM(edge + (inner,), f32),
            pltpu.VMEM(edge + (2 * nstate,), f32),
            pltpu.VMEM(edge + (inner,), f32),
            pltpu.VMEM(edge + (2 * nstate,), f32),
            pltpu.VMEM((tokens, inner), f32),
            pltpu.SMEM((64,), jnp.int32),
            pltpu.VMEM((tokens, PAD), f32),
            pltpu.VMEM((mdl_size, tokens, columns), bf16),
            pltpu.VMEM((8, tokens), f32),
            pltpu.VMEM((mdl_size, tokens, columns), bf16),
            pltpu.VMEM((mdl_size, 8, tokens), f32),
            pltpu.VMEM((per_dev, draft, columns), bf16),
            pltpu.VMEM((SLOTS, draft, columns), bf16),
            pltpu.VMEM((SLOTS, draft, columns), bf16),
            pltpu.SemaphoreType.DMA((16,)),
            pltpu.SemaphoreType.DMA((120,)),
            pltpu.SemaphoreType.DMA((2 + per_dev,)),
        ],
        compiler_params=pltpu.CompilerParams(
            collective_id=0, has_side_effects=True, vmem_limit_bytes=58 << 20
        ),
        name="draft_layer",
    )(
        owner_dev,
        state_page,
        conv_page,
        accepted,
        step_bias,
        decay_log,
        skip_gain,
        z_weight,
        x_weight,
        state_proj,
        step_weight.T,
        out_weight.T,
        conv_inner,
        conv_state,
        norm_gain.reshape(1, -1),
        hist_inner,
        hist_state,
        hidden_in.reshape(per_dev, draft, depth),
        state_pool,
    )
    return (
        mixed.reshape(tokens, columns),
        new_states,
        edge_inner.transpose(1, 0, 2),
        edge_state.transpose(1, 0, 2),
    )


def solution(mesh):
    return jax.shard_map(
        on_device,
        mesh=mesh,
        in_specs=(
            P("req", None),
            P("req", "mdl"),
            P("req", "mdl"),
            P("req", None),
            P("req", "mdl"),
            P("mdl"),
            P("mdl"),
            P("mdl"),
            P(None, "mdl"),
            P(),
            P("mdl"),
            P("mdl", "req"),
            P("req", "mdl", None, None),
            P("req", None, "mdl"),
            P("req", None, None),
            P(),
            P(),
            P(),
            P(),
        ),
        out_specs=(
            P("req", "mdl"),
            P("req", "mdl", None, None),
            P("req", None, "mdl"),
            P("req", None, None),
        ),
        check_vma=False,
    )
```

time: 402 us -> 79.2 us (0.20); the launches traced: 397 us -> 79 us
  waiting for transfers between devices: 206 us -> 0 us
  Pallas kernels: 0 us -> 72.5 us
  blocking collectives: 70.7 us -> 0 us
  starting transfers between devices: 47.6 us -> 0 us
  matrix products: 27.8 us -> 0 us
  between operations: 14.7 us -> 0.65 us
  local copies, waits for them, and re-layouts: 19.2 us -> 5.86 us
  other arithmetic: 10.6 us -> 0 us
    all_gather x4 -> x0, waiting for transfers between devices: 178 us -> none  [the longest x1 82.4 us: project_in(): lax.all_gather(x_weight, 'req', axis=0, tiled=True)]
    pallas_call x0 -> x1, Pallas kernels: none -> 72.5 us  [on_device(): pl.pallas_call(functools.partial(layer_kernel, groups, mdl_size), out_sha...]
    all_gather x1 -> x0, blocking collectives: 57 us -> none  [project_in(): lax.all_gather(step_weight, 'req', axis=0, tiled=True)]
    ppermute x16 -> x0, starting transfers between devices: 47.4 us -> none  [from_behind(): return lax.ppermute(value, axis, pairs)]
    dot_general x15 -> x0, matrix products: 27.8 us -> none  [the longest x4 6.56 us: project_in(): jnp.dot(rows, piece, preferred_element_type=jnp.float32)]
    reduce_scatter x1 -> x0, waiting for transfers between devices: 20.3 us -> none  [finish(): lax.psum_scatter(terms, 'mdl', scatter_dimension=1, tiled=True)]
    psum x1 -> x0, blocking collectives: 13.7 us -> none  [finish(): squares = lax.psum(jnp.sum(gated * gated, axis=1), 'mdl')]
    ppermute x16 -> x0, waiting for transfers between devices: 5.27 us -> none  [from_behind(): return lax.ppermute(value, axis, pairs)]
  transfers between devices with their start and end apart: 21 -> 0, of which waited for: 8 -> 0; matrix products, arithmetic and copies ran while one was open for 13% -> 0% of each run, Pallas kernels for 0% -> 0%
where the time goes in v2:
time: 79.2 us; the launch traced here: 79 us
  Pallas kernels  72.5 us (92%)
  local copies, waits for them, and re-layouts  5.86 us (7%)
    pallas_call x1, Pallas kernels, on_device(): pl.pallas_call(functools.partial(layer_kernel, groups, mdl_size), out_sha...  72.5 us
    unnamed x8, local copies, waits for them, and re-layouts  5.86 us

profile of v2, /device:TPU:1, one launch (start us, length us, event | category | flops | bytes accessed | tf_op | source)
XLA Modules:
  0.0 79.0 jit_solution(15155255922823644091)
XLA Ops:
  0.6 72.5 %draft_layer.1 = (bf16[8,16,256]{2,1,0:T(8,128)(2,1)}, f32[8,8,64,128]{3,2,1,0:T(8,128)}, bf16[3,8,512]{2,1,0:T(8,128)(2,1)}, bf16[3,8,256]{2,1,0:T(8,128)(2,1)}) custom-call(s32[512]{0:T(512)} %owner_dev.1, s32[512]{0:T(512)} %state_page.1, s32[512]{0:T(512)} %conv_page.1, s32[512]{0:T(512)} %accepted.1, f32[8]{0:T(128)} %step_bias.1, f32[8]{0:T(128)} %decay_log.1, ...), custom_call_target="tpu_custom_call" | custom-call | tf_op jit(solution)/shard_map/draft_layer/pallas_call | solution.py:567
  73.1 1.5 %copy.27 = bf16[128,256]{1,0:T(8,128)(2,1)} copy(bf16[128,256]{1,0:T(8,128)(2,1)} %bitcast.10) | data formatting | bytes 131072
  74.6 0.0 copy-start
  74.6 0.0 copy-start.1
  74.6 3.2 %copy.28 = f32[8,8,64,128]{3,2,1,0:T(8,128)} copy(f32[8,8,64,128]{3,2,1,0:T(8,128)} %get-tuple-element.17) | data formatting | bytes 4194304
  77.8 0.0 copy-done
  77.8 0.6 copy.29
  78.4 0.0 copy-done.1
  78.4 0.6 copy.30
Async XLA Ops:
  74.6 3.2 %copy-start = (bf16[3,8,512]{2,1,0:T(8,128)(2,1)S(1)}, bf16[3,8,512]{2,1,0:T(8,128)(2,1)}, u32[]{:S(2)}) copy-start(bf16[3,8,512]{2,1,0:T(8,128)(2,1)} %get-tuple-element.10) | copy-start | bytes 73732
  74.6 3.8 %copy-start.1 = (bf16[3,8,256]{2,1,0:T(8,128)(2,1)S(1)}, bf16[3,8,256]{2,1,0:T(8,128)(2,1)}, u32[]{:S(2)}) copy-start(bf16[3,8,256]{2,1,0:T(8,128)(2,1)} %get-tuple-element.11) | copy-start | bytes 36868

commit v3 on v2

--- a/solution.py
+++ b/solution.py
@@ -15,6 +15,19 @@
 PAD = 128
 HIGH = lax.Precision.HIGHEST
 EPSILON = 1e-05
+
+ORDER = (
+    ("ax", 1), ("ax", 3), ("bu", 1), ("bd", 1), ("ax", 2), ("au", 1, 0), ("ad", 1, 0), ("bl", 0),
+    ("au", 1, 1), ("ad", 1, 1), ("br", 0), ("bl", 1), ("au", 1, 3), ("ad", 1, 3), ("br", 1),
+    ("bl", 2), ("bu", 2), ("bd", 2), ("br", 2), ("au", 1, 2), ("ad", 1, 2), ("bf", 1),
+    ("au", 2, 0), ("ad", 2, 0), ("bf", 0), ("bl", 3), ("au", 2, 1), ("ad", 2, 1), ("br", 3),
+    ("au", 2, 3), ("ad", 2, 3), ("bl", 4), ("br", 4), ("bu", 3), ("bd", 3), ("bf", 3),
+    ("au", 2, 2), ("ad", 2, 2), ("bf", 2), ("au", 3, 0), ("ad", 3, 0), ("bf", 4), ("bl", 5),
+    ("au", 3, 1), ("ad", 3, 1), ("proj", 0), ("proj", 1), ("au", 3, 3), ("ad", 3, 3), ("br", 5),
+    ("bl", 6), ("proj", 2), ("bz", 4), ("proj", 3), ("br", 6), ("bf", 5), ("au", 3, 2),
+    ("ad", 3, 2), ("proj", 4), ("au", 4, 0), ("ad", 4, 3), ("proj", 5), ("br", 7), ("bl", 7),
+    ("au", 4, 1), ("ad", 4, 2), ("bf", 6), ("bf", 7), ("proj", 6), ("proj", 7),
+)
 MESH = pl.DeviceIdType.MESH
 NT = (((1,), (1,)), ((), ()))
 TN = (((0,), (0,)), ((), ()))
@@ -100,6 +113,7 @@
     table,
     decay_s,
     terms,
+    sums,
     squares,
     parts,
     square_parts,
@@ -164,165 +178,6 @@
         step_t[...].astype(f32), place, TN, preferred_element_type=f32, precision=HIGH
     ).astype(bf16)
     full_b[z, x, core, :, inner + PAD :] = out_t[...]
-    pl.semaphore_wait(barrier, len(peers))
-
-    copies = Copies(send_sem, recv_sem, up)
-    half = zn // 2
-    rows = full_a.shape[3]
-    halves = (pl.ds(0, rows // 2), pl.ds(rows // 2, rows // 2))
-    order = [0]
-    for s in range(1, half):
-        order += [-s, s]
-    order.append(-half)
-    place_of = {d: n for n, d in enumerate(order)}
-
-    def piece_a(dz, dx):
-        return full_a.at[zi(z + dz), xi(x + dx), core]
-
-    def piece_b(dz, dx):
-        return full_b.at[zi(z + dz), xi(x + dx), core]
-
-    def a_up(s, d):
-        group = "a_last" if s == half else "a"
-        copies.send(("au", s, d), group, piece_a(1 - s, -d), piece_a(1 - s, -d), up)
-
-    def a_down(s, d):
-        group = "a_last" if s == half else "a"
-        copies.send(("ad", s, d), group, piece_a(s - 1, -d), piece_a(s - 1, -d), down)
-
-    up_last, down_last = range(0, XN // 2), range(XN // 2, XN)
-
-    def b_up(s):
-        p = piece_b(1 - s, 0)
-        if s == half:
-            copies.send(("bu", s), "b_last", p.at[halves[0]], p.at[halves[0]], up)
-        else:
-            copies.send(("bu", s), "b", p, p, up)
-
-    def b_down(s):
-        p = piece_b(s - 1, 0)
-        if s == half:
-            copies.send(("bd", s), "b_last", p.at[halves[1]], p.at[halves[1]], down)
-        else:
-            copies.send(("bd", s), "b", p, p, down)
-
-    def b_side(n):
-        p = piece_b(order[n], 0)
-        copies.send(("br", n), "bx", p, p, right)
-        copies.send(("bl", n), "bx", p, p, left_x)
-
-    def e_ax(d):
-        copies.arrive(("ax", d), "ax", piece_a(0, -d))
-        a_up(1, d)
-        a_down(1, d)
-
-    def e_bz(s):
-        if s < half:
-            copies.arrive(("bu", s), "b", piece_b(-s, 0))
-            b_up(s + 1)
-            b_side(place_of[-s])
-            copies.arrive(("bd", s), "b", piece_b(s, 0))
-            b_down(s + 1)
-            b_side(place_of[s])
-        else:
-            copies.arrive(("bu", s), "b_last", piece_b(-s, 0).at[halves[0]])
-            copies.arrive(("bd", s), "b_last", piece_b(-s, 0).at[halves[1]])
-            b_side(place_of[-s])
-
-    def e_a(s, d):
-        if s < half:
-            copies.arrive(("au", s, d), "a", piece_a(-s, -d))
-            if s + 1 < half or d in up_last:
-                a_up(s + 1, d)
-            copies.arrive(("ad", s, d), "a", piece_a(s, -d))
-            if s + 1 < half or d in down_last:
-                a_down(s + 1, d)
-        elif d in up_last:
-            copies.arrive(("au", s, d), "a_last", piece_a(-s, -d))
-        else:
-            copies.arrive(("ad", s, d), "a_last", piece_a(-s, -d))
-
-    def e_bx(n):
-        copies.arrive(("br", n), "bx", piece_b(order[n], -1))
-        copies.arrive(("bl", n), "bx", piece_b(order[n], 1))
-        if n % 2 == 0:
-            p = piece_b(order[n], -1)
-            copies.send(("bf", n), "bf", p, p, right)
-        else:
-            p = piece_b(order[n], 1)
-            copies.send(("bf", n), "bf", p, p, left_x)
-
-    def e_bf(n):
-        copies.arrive(("bf", n), "bf", piece_b(order[n], 2))
-
-    def e_sib(n):
-        a = full_a.at[zi(z + order[n]), :, core]
-        b = full_b.at[zi(z + order[n]), :, core]
-        copies.send(("sa", n), "sa", a, a, sibling)
-        copies.send(("sb", n), "sb", b, b, sibling)
-
-    def e_proj(n):
-        zz = zi(z + order[n])
-        copies.arrive(("sa", n), "sa", full_a.at[zz, :, 1 - core])
-        copies.arrive(("sb", n), "sb", full_b.at[zz, :, 1 - core])
-        blk = rows_full[zz].reshape(tokens, width)
-        part_a = dot(blk, full_a[zz].reshape(width, full_a.shape[4]))
-        part_b = dot(blk, full_b[zz, :, :, :, : inner + PAD].reshape(width, inner + PAD))
-        if n == 0:
-            acc_a[...] = part_a
-            acc_b[...] = part_b
-        else:
-            acc_a[...] += part_a
-            acc_b[...] += part_b
-
-    def e_rows():
-        for o in range(1, WINDOW):
-            copies.arrive(("h", o), "h", incoming.at[pl.ds(o * CAP, CAP)])
-        by_page = [jnp.int32(0)] * per_dev
-        by_conv = [jnp.int32(0)] * per_dev
-        for o in range(WINDOW):
-            base = ((me - o + groups) % groups) * per_dev
-            seen = jnp.int32(0)
-            pages = [jnp.int32(0)] * CAP
-            for q in range(per_dev):
-                hit = owner_dev[base + q] == me
-                page = jnp.where(hit, state_page[base + q], -1)
-                conv = jnp.where(hit, conv_page[base + q], -1)
-                kept = accepted[base + q]
-                info = (o * CAP + seen) + conv * 64 + kept * 1024
-                back = page + kept * 1024
-                for p in range(per_dev):
-                    by_page[p] = jnp.where(page == p, info, by_page[p])
-                    by_conv[p] = jnp.where(conv == p, back, by_conv[p])
-                for c in range(CAP):
-                    pages[c] = jnp.where(hit & (seen == c), page, pages[c])
-                seen = seen + hit.astype(jnp.int32)
-            for c in range(CAP):
-                table[8 + o * CAP + c] = pages[c]
-        for p in range(per_dev):
-            table[24 + p] = jnp.minimum(by_page[p] & 63, SLOTS - 1)
-            table[32 + p] = jnp.minimum((by_page[p] >> 6) & 15, per_dev - 1)
-            table[40 + p] = jnp.minimum(by_page[p] >> 10, draft)
-            table[48 + p] = jnp.minimum(by_conv[p] & 1023, per_dev - 1)
-            table[56 + p] = jnp.minimum(by_conv[p] >> 10, draft)
-        for p in range(per_dev):
-            rows_full[col, p] = incoming[table[24 + p]]
-        for k in range(1, mdl_size):
-            copies.send(("y", k), "y", rows_full.at[col], rows_full.at[col], across[k - 1])
-
-    def e_rows_in():
-        for k in range(1, mdl_size):
-            copies.arrive(("y", k), "y", rows_full.at[(col - k + mdl_size) % mdl_size])
-
-    own_a, own_b = piece_a(0, 0), piece_b(0, 0)
-    b_up(1)
-    b_down(1)
-    for d in range(1, XN):
-        copies.send(("ax", d), "ax", own_a, own_a, xs[d - 1])
-    b_side(0)
-    a_up(1, 0)
-    a_down(1, 0)
-
     owners = [owner_dev[me * per_dev + q] for q in range(per_dev)]
     slots = []
     for q in range(per_dev):
@@ -339,31 +194,210 @@
         for q in range(per_dev):
             source = jnp.where(slots[q] == s, q, source)
         outgoing[s] = slice_in[source]
+    pl.semaphore_wait(barrier, len(peers))
+
+    copies = Copies(send_sem, recv_sem, up)
+    half = zn // 2
+    rows = full_a.shape[3]
+    halves = (pl.ds(0, rows // 2), pl.ds(rows // 2, rows // 2))
+    order = [0]
+    for s in range(1, half):
+        order += [-s, s]
+    order.append(-half)
+    place_of = {d: n for n, d in enumerate(order)}
+
+    def piece_a(dz, dx):
+        return full_a.at[zi(z + dz), xi(x + dx), core]
+
+    def piece_b(dz, dx):
+        return full_b.at[zi(z + dz), xi(x + dx), core]
+
+    def share_a(dz, dx):
+        p = piece_a(dz, dx)
+        copies.send(("sa", place_of[dz]), "sa", p, p, sibling)
+
+    def share_b(dz, dx):
+        p = piece_b(dz, dx)
+        copies.send(("sb", place_of[dz]), "sb", p, p, sibling)
+
+    def a_up(s, d):
+        group = "a_last" if s == half else "a"
+        copies.send(("au", s, d), group, piece_a(1 - s, -d), piece_a(1 - s, -d), up)
+
+    def a_down(s, d):
+        group = "a_last" if s == half else "a"
+        copies.send(("ad", s, d), group, piece_a(s - 1, -d), piece_a(s - 1, -d), down)
+
+    up_last, down_last = range(0, XN // 2), range(XN // 2, XN)
+
+    def b_up(s):
+        p = piece_b(1 - s, 0)
+        if s == half:
+            copies.send(("bu", s), "b_last", p.at[halves[0]], p.at[halves[0]], up)
+        else:
+            copies.send(("bu", s), "b", p, p, up)
+
+    def b_down(s):
+        p = piece_b(s - 1, 0)
+        if s == half:
+            copies.send(("bd", s), "b_last", p.at[halves[1]], p.at[halves[1]], down)
+        else:
+            copies.send(("bd", s), "b", p, p, down)
+
+    def b_side(n):
+        p = piece_b(order[n], 0)
+        copies.send(("br", n), "bx", p, p, right)
+        copies.send(("bl", n), "bx", p, p, left_x)
+
+    def e_ax(d):
+        copies.arrive(("ax", d), "ax", piece_a(0, -d))
+        a_up(1, d)
+        a_down(1, d)
+        share_a(0, -d)
+
+    def e_bu(s):
+        copies.arrive(("bu", s), "b", piece_b(-s, 0))
+        b_up(s + 1)
+        b_side(place_of[-s])
+        share_b(-s, 0)
+
+    def e_bd(s):
+        copies.arrive(("bd", s), "b", piece_b(s, 0))
+        b_down(s + 1)
+        b_side(place_of[s])
+        share_b(s, 0)
+
+    def e_bz(s):
+        copies.arrive(("bu", s), "b_last", piece_b(-s, 0).at[halves[0]])
+        copies.arrive(("bd", s), "b_last", piece_b(-s, 0).at[halves[1]])
+        b_side(place_of[-s])
+        share_b(-s, 0)
+
+    def e_au(s, d):
+        copies.arrive(("au", s, d), "a" if s < half else "a_last", piece_a(-s, -d))
+        if s + 1 < half or (s < half and d in up_last):
+            a_up(s + 1, d)
+        share_a(-s, -d)
+
+    def e_ad(s, d):
+        copies.arrive(("ad", s, d), "a" if s < half else "a_last", piece_a(s, -d))
+        if s + 1 < half or (s < half and d in down_last):
+            a_down(s + 1, d)
+        share_a(s if s < half else -s, -d)
+
+    def e_br(n):
+        p = piece_b(order[n], -1)
+        copies.arrive(("br", n), "bx", p)
+        if n % 2 == 0:
+            copies.send(("bf", n), "bf", p, p, right)
+        share_b(order[n], -1)
+
+    def e_bl(n):
+        p = piece_b(order[n], 1)
+        copies.arrive(("bl", n), "bx", p)
+        if n % 2 == 1:
+            copies.send(("bf", n), "bf", p, p, left_x)
+        share_b(order[n], 1)
+
+    def e_bf(n):
+        copies.arrive(("bf", n), "bf", piece_b(order[n], 2))
+        share_b(order[n], 2)
+
+    def e_proj(n):
+        zz = zi(z + order[n])
+        copies.arrive(("sa", n), "sa", full_a.at[zz, :, 1 - core])
+        copies.arrive(("sb", n), "sb", full_b.at[zz, :, 1 - core])
+        blk = rows_full[zz].reshape(tokens, width)
+        part_a = dot(blk, full_a[zz].reshape(width, full_a.shape[4]))
+        part_b = dot(blk, full_b[zz, :, :, :, : inner + PAD].reshape(width, inner + PAD))
+        if n == 0:
+            acc_a[...] = part_a
+            acc_b[...] = part_b
+        else:
+            acc_a[...] += part_a
+            acc_b[...] += part_b
+
+    def e_table(o):
+        base = ((me - o + groups) % groups) * per_dev
+        seen = jnp.int32(0)
+        pages = [jnp.int32(0)] * CAP
+        for q in range(per_dev):
+            hit = owner_dev[base + q] == me
+            page = jnp.where(hit, state_page[base + q], -1)
+            conv = jnp.where(hit, conv_page[base + q], -1)
+            kept = accepted[base + q]
+            info = (o * CAP + seen) + conv * 64 + kept * 1024
+            back = page + kept * 1024
+            for p in range(per_dev):
+                by_page[p] = jnp.where(page == p, info, by_page[p])
+                by_conv[p] = jnp.where(conv == p, back, by_conv[p])
+            for c in range(CAP):
+                pages[c] = jnp.where(hit & (seen == c), page, pages[c])
+            seen = seen + hit.astype(jnp.int32)
+        for c in range(CAP):
+            table[8 + o * CAP + c] = pages[c]
+
+    by_page = [jnp.int32(0)] * per_dev
+    by_conv = [jnp.int32(0)] * per_dev
+
+    def e_rows():
+        for o in range(1, WINDOW):
+            copies.arrive(("h", o), "h", incoming.at[pl.ds(o * CAP, CAP)])
+        for p in range(per_dev):
+            table[24 + p] = jnp.minimum(by_page[p] & 63, SLOTS - 1)
+            table[32 + p] = jnp.minimum((by_page[p] >> 6) & 15, per_dev - 1)
+            table[40 + p] = jnp.minimum(by_page[p] >> 10, draft)
+            table[48 + p] = jnp.minimum(by_conv[p] & 1023, per_dev - 1)
+            table[56 + p] = jnp.minimum(by_conv[p] >> 10, draft)
+        for p in range(per_dev):
+            rows_full[col, p] = incoming[table[24 + p]]
+        for k in range(1, mdl_size):
+            copies.send(("y", k), "y", rows_full.at[col], rows_full.at[col], across[k - 1])
+
+    def e_rows_in():
+        for k in range(1, mdl_size):
+            copies.arrive(("y", k), "y", rows_full.at[(col - k + mdl_size) % mdl_size])
+
     for o in range(1, WINDOW):
         part = pl.ds(o * CAP, CAP)
         copies.send(("h", o), "h", outgoing.at[part], incoming.at[part], ahead[o - 1])
     incoming[0:CAP] = outgoing[0:CAP]
 
-    events = []
-    for d, t in ((1, 2.0), (3, 2.1), (2, 3.0)):
-        events.append((t, "ax", functools.partial(e_ax, d)))
-    for s in range(1, half + 1):
-        events.append((0.4 + 2.2 * s, "bz", functools.partial(e_bz, s)))
-        for j, d in enumerate((0, 1, 3, 2)):
-            events.append((2.6 + 5.0 * (s - 1) + 1.2 * j, "a", functools.partial(e_a, s, d)))
-    for n in range(zn):
-        t_bx = 3.4 + 2.2 * n
-        t_a = 4.0 if n == 0 else 6.3 + 5.0 * (abs(order[n]) - 1)
-        t_sib = max(t_bx + 2.5, t_a + 0.01)
-        events.append((t_bx, "bx", functools.partial(e_bx, n)))
-        events.append((t_bx + 2.5, "bf", functools.partial(e_bf, n)))
-        events.append((t_sib + 0.02, "sib", functools.partial(e_sib, n)))
-        events.append((max(t_sib + 2.0, 16.0), "proj", functools.partial(e_proj, n)))
-    events.append((4.5, "rows", e_rows))
-    events.append((15.9, "in", e_rows_in))
-    events.sort(key=lambda e: e[0])
-    for _, _, run in events:
-        run()
+    own_a, own_b = piece_a(0, 0), piece_b(0, 0)
+    b_up(1)
+    b_down(1)
+    for d in range(1, XN):
+        copies.send(("ax", d), "ax", own_a, own_a, xs[d - 1])
+    a_up(1, 0)
+    a_down(1, 0)
+    b_side(0)
+    share_a(0, 0)
+    share_b(0, 0)
+
+
+    run = {
+        "ax": e_ax,
+        "bu": e_bu,
+        "bd": e_bd,
+        "bz": e_bz,
+        "au": e_au,
+        "ad": e_ad,
+        "br": e_br,
+        "bl": e_bl,
+        "bf": e_bf,
+        "proj": e_proj,
+    }
+    for o in range(WINDOW):
+        e_table(o)
+    started, projected = False, False
+    for event in ORDER:
+        if event[0] == "au" and not started:
+            started = True
+            e_rows()
+        if event[0] == "proj" and not projected:
+            projected = True
+            e_rows_in()
+        run[event[0]](*event[1:])
 
     hist_x[...] = hist_inner[...].astype(f32)
     hist_s[...] = hist_state[...].astype(f32)
@@ -413,12 +447,14 @@
 
     b_low = b_rows.astype(bf16)
     c_low = c_rows.astype(bf16)
+    c_rest = (c_rows - c_low.astype(f32)).astype(bf16)
     load_state.wait()
     for p in range(per_dev):
         start = state[p].reshape(inner, nstate)
-        carried[p * draft : (p + 1) * draft, :] = dot_nt(
-            c_low[p * draft : (p + 1) * draft, :], start.astype(bf16)
-        )
+        mine = slice(p * draft, (p + 1) * draft)
+        both = jnp.concatenate([c_low[mine], c_rest[mine]], axis=0)
+        found = dot_nt(both, start.astype(bf16))
+        carried[mine, :] = found[:draft] + found[draft:]
 
     left = lax.broadcasted_iota(jnp.int32, (tokens, PAD), 1) < hdim
 
@@ -431,11 +467,14 @@
         cols = slice(j * PAD, (j + 1) * PAD)
         x_pair = active[:, cols]
         x_low = x_pair.astype(bf16)
+        x_rest = (x_pair - x_low.astype(f32)).astype(bf16)
         pair = []
         for h in (2 * j, 2 * j + 1):
             gap = decay[:, h : h + 1] - decay_t[h : h + 1, :]
             weight = jnp.exp(jnp.where(causal, gap, -1e30)) * scores * size_t[h : h + 1, :]
-            pair.append(dot(weight.astype(bf16), x_low))
+            w_low = weight.astype(bf16)
+            w_rest = (weight - w_low.astype(f32)).astype(bf16)
+            pair.append(dot(w_low, x_low) + dot(w_rest, x_low) + dot(w_low, x_rest))
         skip = jnp.where(left, skip_gain[2 * j], skip_gain[2 * j + 1])
         y = (
             jnp.where(left, pair[0], pair[1])
@@ -449,17 +488,26 @@
     squares[...] = dot_nt(jnp.ones((8, PAD), f32), total, HIGH)
     for k in range(1, mdl_size):
         copies.send(("s", k), "s", squares, square_parts.at[k], across[k - 1])
-    far_first = sorted(range(1, mdl_size), key=lambda k: -min(k, mdl_size - k))
-
-    def project_out(m):
+
+    def project_out(k):
+        m = (col + k + mdl_size) % mdl_size
         block = full_b[m, :, :, :, inner + PAD :].reshape(columns, inner)
         return dot_nt(gated_low, block)
 
-    for k in far_first:
-        m = (col + k) % mdl_size
-        terms[k] = project_out(m).astype(bf16)
-        copies.send(("t", k), "t", terms.at[k], parts.at[k], across[k - 1])
-    own_term = project_out(col)
+    def ring(k):
+        return across[k % mdl_size - 1]
+
+    low, high = pl.ds(0, tokens // 2), pl.ds(tokens // 2, tokens // 2)
+    terms[4] = project_out(4).astype(bf16)
+    copies.send(("t4u",), "t", terms.at[4, low], parts.at[2, low], ring(2))
+    copies.send(("t4d",), "t", terms.at[4, high], parts.at[2, high], ring(-2))
+    for k, name, slot in ((3, "t3u", 0), (-3, "t3d", 1), (1, "t1u", 3), (-1, "t1d", 4)):
+        terms[k % mdl_size] = project_out(k).astype(bf16)
+        towards = 1 if k > 0 else -1
+        copies.send((name,), "t", terms.at[k % mdl_size], parts.at[slot], ring(towards))
+    sums[0] = project_out(2)
+    sums[1] = project_out(-2)
+    own_term = project_out(0)
 
     picked_t = []
     for j in range(heads // 2):
@@ -476,6 +524,18 @@
         store = pltpu.make_async_copy(state.at[p], new_states.at[p], local_sem.at[2 + p])
         store.start()
         stores.append(store)
+    copies.arrive(("t3u",), "t", parts.at[0])
+    copies.arrive(("t4u",), "t", parts.at[2, low])
+    sums[0] += parts[0].astype(f32)
+    sums[0, low, :] += parts[2, low, :].astype(f32)
+    terms[2] = sums[0].astype(bf16)
+    copies.send(("t2u",), "t", terms.at[2], parts.at[5], ring(2))
+    copies.arrive(("t3d",), "t", parts.at[1])
+    copies.arrive(("t4d",), "t", parts.at[2, high])
+    sums[1] += parts[1].astype(f32)
+    sums[1, high, :] += parts[2, high, :].astype(f32)
+    terms[mdl_size - 2] = sums[1].astype(bf16)
+    copies.send(("t2d",), "t", terms.at[mdl_size - 2], parts.at[6], ring(-2))
     for c in range(per_dev):
         for j in range(KCONV - 1):
             row = pl.ds(lead + table[56 + c] + j, 1)
@@ -493,9 +553,9 @@
         stacked, eighth, TN, preferred_element_type=f32, precision=HIGH
     ) / (mdl_size * inner)
     scale = lax.rsqrt(mean + EPSILON)
-    for k in reversed(far_first):
-        copies.arrive(("t", k), "t", parts.at[k])
-        own_term = own_term + parts[k].astype(f32)
+    for name, slot in (("t1u", 3), ("t1d", 4), ("t2u", 5), ("t2d", 6)):
+        copies.arrive((name,), "t", parts.at[slot])
+        own_term = own_term + parts[slot].astype(f32)
     result[...] = (own_term * scale).astype(bf16).reshape(per_dev, draft, columns)
     for s in range(SLOTS):
         outgoing2[s] = result[table[8 + s]]
@@ -524,6 +584,32 @@
     for q in range(per_dev):
         mixed[q] = incoming2[table[q]]
     copies.sent("r", incoming2.at[pl.ds(CAP, SLOTS - CAP)])
+
+
+def store_kernel(mixed, states, edge_inner, edge_state, *outs):
+    for source, out in zip((mixed, states, edge_inner, edge_state), outs, strict=True):
+        out[...] = source[...]
+
+
+def store(mixed, states, edge_inner, edge_state):
+    steps = 4
+    chunk = (states.shape[0] // steps,) + states.shape[1:]
+    state_spec = pl.BlockSpec(chunk, lambda k: (k, 0, 0, 0))
+
+    def whole(a):
+        return pl.BlockSpec(a.shape, lambda k: (0,) * len(a.shape))
+
+    specs = (whole(mixed), state_spec, whole(edge_inner), whole(edge_state))
+    arrays = (mixed, states, edge_inner, edge_state)
+    return pl.pallas_call(
+        store_kernel,
+        grid=(steps,),
+        out_shape=tuple(jax.ShapeDtypeStruct(a.shape, a.dtype) for a in arrays),
+        in_specs=list(specs),
+        out_specs=specs,
+        compiler_params=pltpu.CompilerParams(vmem_limit_bytes=60 << 20),
+        name="store_results",
+    )(*arrays)
 
 
 def on_device(
@@ -594,6 +680,7 @@
             pltpu.SMEM((64,), jnp.int32),
             pltpu.VMEM((tokens, PAD), f32),
             pltpu.VMEM((mdl_size, tokens, columns), bf16),
+            pltpu.VMEM((2, tokens, columns), f32),
             pltpu.VMEM((8, tokens), f32),
             pltpu.VMEM((mdl_size, tokens, columns), bf16),
             pltpu.VMEM((mdl_size, 8, tokens), f32),
@@ -629,6 +716,9 @@
         hidden_in.reshape(per_dev, draft, depth),
         state_pool,
     )
+    mixed, new_states, edge_inner, edge_state = store(
+        mixed, new_states, edge_inner, edge_state
+    )
     return (
         mixed.reshape(tokens, columns),
         new_states,

time: 79.2 us -> 71.7 us (0.905)
  local copies, waits for them, and re-layouts: 5.86 us -> 0 us
  Pallas kernels: 72.5 us -> 70.8 us
    unnamed x8 -> x0, local copies, waits for them, and re-layouts: 5.86 us -> none
    pallas_call x1, Pallas kernels: 72.5 us -> 66.9 us  [on_device(): pl.pallas_call(functools.partial(layer_kernel, groups, mdl_size), out_sha...]
    pallas_call x0 -> x1, Pallas kernels: none -> 3.84 us  [store(): pl.pallas_call(store_kernel, grid=(steps,), out_shape=tuple((jax.ShapeDty...]
where the time goes in v3:
time: 71.7 us; the launch traced here: 71.4 us
  Pallas kernels  70.8 us (99%)
    pallas_call x1, Pallas kernels, on_device(): pl.pallas_call(functools.partial(layer_kernel, groups, mdl_size), out_sha...  66.9 us
    pallas_call x1, Pallas kernels, store(): pl.pallas_call(store_kernel, grid=(steps,), out_shape=tuple((jax.ShapeDty...  3.84 us

profile of v3, /device:TPU:1, one launch (start us, length us, event | category | flops | bytes accessed | tf_op | source)
XLA Modules:
  0.0 71.4 jit_solution(1951472345521231314)
XLA Ops:
  0.6 66.9 %draft_layer.1 = (bf16[8,16,256]{2,1,0:T(8,128)(2,1)}, f32[8,8,64,128]{3,2,1,0:T(8,128)}, bf16[3,8,512]{2,1,0:T(8,128)(2,1)}, bf16[3,8,256]{2,1,0:T(8,128)(2,1)}) custom-call(s32[512]{0:T(512)} %owner_dev.1, s32[512]{0:T(512)} %state_page.1, s32[512]{0:T(512)} %conv_page.1, s32[512]{0:T(512)} %accepted.1, f32[8]{0:T(128)} %step_bias.1, f32[8]{0:T(128)} %decay_log.1, ...), custom_call_target="tpu_custom_call" | custom-call | tf_op jit(solution)/shard_map/draft_layer/pallas_call | solution.py:653
  67.6 3.8 %store_results.1 = (bf16[8,16,256]{2,1,0:T(8,128)(2,1)}, f32[8,8,64,128]{3,2,1,0:T(8,128)}, bf16[3,8,512]{2,1,0:T(8,128)(2,1)}, bf16[3,8,256]{2,1,0:T(8,128)(2,1)}) custom-call(bf16[8,16,256]{2,1,0:T(8,128)(2,1)} %get-tuple-element.12.mixed, f32[8,8,64,128]{3,2,1,0:T(8,128)} %get-tuple-element.13.states, bf16[3,8,512]{2,1,0:T(8,128)(2,1)} %get-tuple-element.14.edge_inner, ...), custom_call_target="tpu_custom_call" | custom-call | tf_op jit(solution)/shard_map/store_results/pallas_call | solution.py:604

commit v4 on v3

--- a/solution.py
+++ b/solution.py
@@ -101,6 +101,7 @@
     outgoing,
     incoming,
     state,
+    state_low,
     acc_a,
     acc_b,
     series_x,
@@ -389,8 +390,21 @@
     }
     for o in range(WINDOW):
         e_table(o)
+    lead = 8 - (KCONV - 1)
+
+    def e_state(p):
+        state_low[p] = state[p].reshape(inner, nstate).astype(bf16)
+
+    def e_history():
+        hist_x[...] = hist_inner[...].astype(f32)
+        hist_s[...] = hist_state[...].astype(f32)
+        for p in range(per_dev):
+            for j in range(KCONV - 1):
+                series_x[p, lead + j : lead + j + 1, :] = hist_x[j, pl.ds(table[32 + p], 1), :]
+                series_s[p, lead + j : lead + j + 1, :] = hist_s[j, pl.ds(table[32 + p], 1), :]
+
     started, projected = False, False
-    for event in ORDER:
+    for n, event in enumerate(ORDER):
         if event[0] == "au" and not started:
             started = True
             e_rows()
@@ -398,18 +412,17 @@
             projected = True
             e_rows_in()
         run[event[0]](*event[1:])
-
-    hist_x[...] = hist_inner[...].astype(f32)
-    hist_s[...] = hist_state[...].astype(f32)
-    lead = 8 - (KCONV - 1)
+        if n == 11:
+            load_state.wait()
+        if 12 <= n < 12 + 2 * per_dev and n % 2 == 0:
+            e_state((n - 12) // 2)
+        if n == 13:
+            e_history()
+
     series_x[:, 8:, :] = acc_b[:, :inner].astype(bf16).astype(f32).reshape(per_dev, draft, inner)
     series_s[:, 8:, :] = (
         acc_a[:, inner:].astype(bf16).astype(f32).reshape(per_dev, draft, 2 * nstate)
     )
-    for p in range(per_dev):
-        for j in range(KCONV - 1):
-            series_x[p, lead + j : lead + j + 1, :] = hist_x[j, pl.ds(table[32 + p], 1), :]
-            series_s[p, lead + j : lead + j + 1, :] = hist_s[j, pl.ds(table[32 + p], 1), :]
 
     def conv(series, taps):
         total = taps[0:1, :] * series[:, lead : lead + draft, :]
@@ -448,12 +461,10 @@
     b_low = b_rows.astype(bf16)
     c_low = c_rows.astype(bf16)
     c_rest = (c_rows - c_low.astype(f32)).astype(bf16)
-    load_state.wait()
     for p in range(per_dev):
-        start = state[p].reshape(inner, nstate)
         mine = slice(p * draft, (p + 1) * draft)
         both = jnp.concatenate([c_low[mine], c_rest[mine]], axis=0)
-        found = dot_nt(both, start.astype(bf16))
+        found = dot_nt(both, state_low[p])
         carried[mine, :] = found[:draft] + found[draft:]
 
     left = lax.broadcasted_iota(jnp.int32, (tokens, PAD), 1) < hdim
@@ -586,27 +597,40 @@
     copies.sent("r", incoming2.at[pl.ds(CAP, SLOTS - CAP)])
 
 
-def store_kernel(mixed, states, edge_inner, edge_state, *outs):
-    for source, out in zip((mixed, states, edge_inner, edge_state), outs, strict=True):
-        out[...] = source[...]
-
-
-def store(mixed, states, edge_inner, edge_state):
-    steps = 4
-    chunk = (states.shape[0] // steps,) + states.shape[1:]
-    state_spec = pl.BlockSpec(chunk, lambda k: (k, 0, 0, 0))
-
-    def whole(a):
-        return pl.BlockSpec(a.shape, lambda k: (0,) * len(a.shape))
-
-    specs = (whole(mixed), state_spec, whole(edge_inner), whole(edge_state))
-    arrays = (mixed, states, edge_inner, edge_state)
+def store_kernel(mixed, states, edge_inner, edge_state, *refs):
+    outs, held, sems = refs[:4], refs[4:8], refs[8]
+    parts = [(states.at[p], outs[1].at[p], held[1].at[p]) for p in range(states.shape[0])]
+    for source, out, hold in (
+        (mixed, outs[0], held[0]),
+        (edge_inner, outs[2], held[2]),
+        (edge_state, outs[3], held[3]),
+    ):
+        parts.append((source, out, hold))
+    loads = [
+        pltpu.make_async_copy(source, hold, sems.at[0, i])
+        for i, (source, _, hold) in enumerate(parts)
+    ]
+    stores = [
+        pltpu.make_async_copy(hold, out, sems.at[1, i]) for i, (_, out, hold) in enumerate(parts)
+    ]
+    for load in loads:
+        load.start()
+    for load, store in zip(loads, stores, strict=True):
+        load.wait()
+        store.start()
+    for store in stores:
+        store.wait()
+
+
+def store(*arrays):
+    hbm = pl.BlockSpec(memory_space=pl.ANY)
     return pl.pallas_call(
         store_kernel,
-        grid=(steps,),
         out_shape=tuple(jax.ShapeDtypeStruct(a.shape, a.dtype) for a in arrays),
-        in_specs=list(specs),
-        out_specs=specs,
+        in_specs=[hbm] * 4,
+        out_specs=(hbm,) * 4,
+        scratch_shapes=[pltpu.VMEM(a.shape, a.dtype) for a in arrays]
+        + [pltpu.SemaphoreType.DMA((2, arrays[1].shape[0] + 3))],
         compiler_params=pltpu.CompilerParams(vmem_limit_bytes=60 << 20),
         name="store_results",
     )(*arrays)
@@ -668,6 +692,7 @@
             pltpu.VMEM((SLOTS, draft, width), bf16),
             pltpu.VMEM((SLOTS, draft, width), bf16),
             pltpu.VMEM(state_pool.shape, f32),
+            pltpu.VMEM((per_dev, inner, nstate), bf16),
             pltpu.VMEM((tokens, inner + 2 * nstate), f32),
             pltpu.VMEM((tokens, inner + PAD), f32),
             pltpu.VMEM((per_dev, draft + 8, inner), f32),

time: 71.7 us -> 70.1 us (0.978)
  Pallas kernels: 70.8 us -> 69.2 us
    pallas_call x1, Pallas kernels: 3.84 us -> 2.47 us  [store(): pl.pallas_call(store_kernel, out_shape=tuple((jax.ShapeDtypeStruct(a.shap...]
where the time goes in v4:
time: 70.1 us; the launch traced here: 69.8 us
  Pallas kernels  69.2 us (99%)
    pallas_call x1, Pallas kernels, on_device(): pl.pallas_call(functools.partial(layer_kernel, groups, mdl_size), out_sha...  66.7 us
    pallas_call x1, Pallas kernels, store(): pl.pallas_call(store_kernel, out_shape=tuple((jax.ShapeDtypeStruct(a.shap...  2.47 us

profile of v4, /device:TPU:1, one launch (start us, length us, event | category | flops | bytes accessed | tf_op | source)
XLA Modules:
  0.0 69.8 jit_solution(12097517525702332206)
XLA Ops:
  0.6 66.7 %draft_layer.1 = (bf16[8,16,256]{2,1,0:T(8,128)(2,1)}, f32[8,8,64,128]{3,2,1,0:T(8,128)}, bf16[3,8,512]{2,1,0:T(8,128)(2,1)}, bf16[3,8,256]{2,1,0:T(8,128)(2,1)}) custom-call(s32[512]{0:T(512)} %owner_dev.1, s32[512]{0:T(512)} %state_page.1, s32[512]{0:T(512)} %conv_page.1, s32[512]{0:T(512)} %accepted.1, f32[8]{0:T(128)} %step_bias.1, f32[8]{0:T(128)} %decay_log.1, ...), custom_call_target="tpu_custom_call" | custom-call | tf_op jit(solution)/shard_map/draft_layer/pallas_call | solution.py:677
  67.4 2.5 %store_results.1 = (bf16[8,16,256]{2,1,0:T(8,128)(2,1)}, f32[8,8,64,128]{3,2,1,0:T(8,128)}, bf16[3,8,512]{2,1,0:T(8,128)(2,1)}, bf16[3,8,256]{2,1,0:T(8,128)(2,1)}) custom-call(bf16[8,16,256]{2,1,0:T(8,128)(2,1)} %get-tuple-element.12.mixed, f32[8,8,64,128]{3,2,1,0:T(8,128)} %get-tuple-element.13.states, bf16[3,8,512]{2,1,0:T(8,128)(2,1)} %get-tuple-element.14.edge_inner, ...), custom_call_target="tpu_custom_call" | custom-call | tf_op jit(solution)/shard_map/store_results/pallas_call | solution.py:627

commit v5 on v4

--- a/solution.py
+++ b/solution.py
@@ -496,9 +496,6 @@
         total = total + gated * gated
         gated_cols.append((gated * norm_gain[0:1, cols]).astype(bf16))
     gated_low = jnp.concatenate(gated_cols, axis=1)
-    squares[...] = dot_nt(jnp.ones((8, PAD), f32), total, HIGH)
-    for k in range(1, mdl_size):
-        copies.send(("s", k), "s", squares, square_parts.at[k], across[k - 1])
 
     def project_out(k):
         m = (col + k + mdl_size) % mdl_size
@@ -516,6 +513,9 @@
         terms[k % mdl_size] = project_out(k).astype(bf16)
         towards = 1 if k > 0 else -1
         copies.send((name,), "t", terms.at[k % mdl_size], parts.at[slot], ring(towards))
+    squares[...] = dot_nt(jnp.ones((8, PAD), f32), total, HIGH)
+    for k in range(1, mdl_size):
+        copies.send(("s", k), "s", squares, square_parts.at[k], across[k - 1])
     sums[0] = project_out(2)
     sums[1] = project_out(-2)
     own_term = project_out(0)

time: 70.1 us -> 69.3 us (0.989)
  Pallas kernels: 69.2 us -> 68.4 us
    pallas_call x1, Pallas kernels: 66.7 us -> 66 us  [on_device(): pl.pallas_call(functools.partial(layer_kernel, groups, mdl_size), out_sha...]
where the time goes in v5:
time: 69.3 us; the launch traced here: 69.1 us
  Pallas kernels  68.4 us (99%)
    pallas_call x1, Pallas kernels, on_device(): pl.pallas_call(functools.partial(layer_kernel, groups, mdl_size), out_sha...  66 us
    pallas_call x1, Pallas kernels, store(): pl.pallas_call(store_kernel, out_shape=tuple((jax.ShapeDtypeStruct(a.shap...  2.47 us

profile of v5, /device:TPU:1, one launch (start us, length us, event | category | flops | bytes accessed | tf_op | source)
XLA Modules:
  0.0 69.1 jit_solution(16001279076747712524)
XLA Ops:
  0.6 66.0 %draft_layer.1 = (bf16[8,16,256]{2,1,0:T(8,128)(2,1)}, f32[8,8,64,128]{3,2,1,0:T(8,128)}, bf16[3,8,512]{2,1,0:T(8,128)(2,1)}, bf16[3,8,256]{2,1,0:T(8,128)(2,1)}) custom-call(s32[512]{0:T(512)} %owner_dev.1, s32[512]{0:T(512)} %state_page.1, s32[512]{0:T(512)} %conv_page.1, s32[512]{0:T(512)} %accepted.1, f32[8]{0:T(128)} %step_bias.1, f32[8]{0:T(128)} %decay_log.1, ...), custom_call_target="tpu_custom_call" | custom-call | tf_op jit(solution)/shard_map/draft_layer/pallas_call | solution.py:677
  66.6 2.5 %store_results.1 = (bf16[8,16,256]{2,1,0:T(8,128)(2,1)}, f32[8,8,64,128]{3,2,1,0:T(8,128)}, bf16[3,8,512]{2,1,0:T(8,128)(2,1)}, bf16[3,8,256]{2,1,0:T(8,128)(2,1)}) custom-call(bf16[8,16,256]{2,1,0:T(8,128)(2,1)} %get-tuple-element.12.mixed, f32[8,8,64,128]{3,2,1,0:T(8,128)} %get-tuple-element.13.states, bf16[3,8,512]{2,1,0:T(8,128)(2,1)} %get-tuple-element.14.edge_inner, ...), custom_call_target="tpu_custom_call" | custom-call | tf_op jit(solution)/shard_map/store_results/pallas_call | solution.py:627
